TPU v7x, 128 devices: a whole 4x4x4 slice. The times are simulated.
128 devices in a mesh: cam: 32 (over x, z_lo, y), band: 4 (over z_hi, core).
Axes of the slice: x: 4, y: 4, z: 4 (z_hi: 2, z_lo: 2; z = z_hi * 2 + z_lo), core: 2. Of those that a mesh axis runs over, the one named last changes fastest.
Arguments:
- images: bfloat16 [32, 128, 64, 512], P('cam', None, 'band'), may hold values from -6 to 6
- weight: bfloat16 [3, 3, 256, 128], replicated, may hold values from -0.1875 to 0.1875
- offsets: int32 [32], replicated, may hold values from 0 to 127
- cotangent: bfloat16 [32, 64, 512, 128], P('cam', 'band'), may hold values from -6 to 6
Outputs:
- image_grad: float32 [32, 128, 64, 512], P('cam', None, 'band')
- weight_grad: float32 [3, 3, 256, 128], replicated
All inputs are finite; a program needn't handle non-finite values.
Results may differ from a plain program's by a relative error of at most 0.0085.
Values may be sent and summed in bfloat16 or wider, within the bound.
No kernel may reach another device: no remote copies, remote signals or barrier semaphores. Data moves between devices by JAX's collectives and lax.ppermute only.
A program may use at most 192 MiB of HBM per device.

v0:
```python
import math

import jax
import jax.numpy as jnp
from jax import lax
from jax.experimental import pallas as pl
from jax.experimental.pallas import tpu as pltpu
from jax.sharding import PartitionSpec as P

C_IN = 128
C_OUT = 256
DISP = 128
F32 = jnp.float32
BF16 = jnp.bfloat16
MIB = 1024 * 1024


def params(limit_mib):
    return pltpu.CompilerParams(
        dimension_semantics=("arbitrary",), vmem_limit_bytes=limit_mib * MIB
    )


def without_lane(tile, place):
    lane = lax.broadcasted_iota(jnp.int32, tile.shape, 1)
    return jnp.where(lane == place, 0.0, tile)


def shifted_right(x):
    moved = pltpu.roll(x, 1, 1)
    return jnp.concatenate([without_lane(moved[:, :DISP], 0), moved[:, DISP:]], axis=1)


def shifted_left(x):
    width = x.shape[1]
    moved = pltpu.roll(x, width - 1, 1)
    return jnp.concatenate(
        [moved[:, : width - DISP], without_lane(moved[:, width - DISP :], DISP - 1)], axis=1
    )


def put_taps(taps_ref, place, row):
    wide = row.astype(F32)
    taps_ref[place, :C_IN, :] = shifted_right(wide).astype(BF16)
    taps_ref[place, C_IN : 2 * C_IN, :] = row
    taps_ref[place, 2 * C_IN :, :] = shifted_left(wide).astype(BF16)


def next_row(taps_ref, x_ref, r):
    @pl.when(r == 0)
    def _():
        put_taps(taps_ref, 1, x_ref[0])
        put_taps(taps_ref, 2, x_ref[1])

    taps_ref[0] = taps_ref[1]
    taps_ref[1] = taps_ref[2]
    put_taps(taps_ref, 2, x_ref[r + 2])


def conv_row(weight_ref, taps_ref):
    patch = taps_ref[...].reshape(9 * C_IN, taps_ref.shape[2])
    return jnp.dot(weight_ref[...], patch, preferred_element_type=F32)


def own_kernel(x_ref, weight_ref, cot_ref, feat_ref, featt_ref, skew_ref, tap_ref, taps):
    r = pl.program_id(0)

    next_row(taps, x_ref, r)
    feat = conv_row(weight_ref, taps)
    feat_ref[0] = feat.astype(BF16)
    featt_ref[0] = feat.T.astype(BF16)
    tap_ref[0] = taps[1]
    rows = lax.broadcasted_iota(jnp.int32, (DISP, DISP), 0)
    cols = lax.broadcasted_iota(jnp.int32, (DISP, DISP), 1)
    exchange = jnp.where(rows + cols == DISP - 1, 1.0, 0.0).astype(BF16)
    flipped = jnp.dot(cot_ref[0], exchange, preferred_element_type=F32)
    blocks = flipped.shape[0] // DISP
    for b in range(blocks):
        part = flipped[b * DISP : (b + 1) * DISP]
        wide = jnp.concatenate([part, jnp.zeros_like(part)], axis=1)
        skew_ref[0, b * DISP : (b + 1) * DISP] = pltpu.roll(
            wide, 0, 1, stride=1, stride_axis=0
        ).astype(BF16)


def own_side(x_haloed, weight_fwd, cot_haloed):
    rows, columns, _ = cot_haloed.shape
    row = lambda *tail: pl.BlockSpec((1,) + tail, lambda r: (r,) + (0,) * len(tail))
    return pl.pallas_call(
        own_kernel,
        grid=(rows,),
        in_specs=[
            pl.BlockSpec(x_haloed.shape, lambda r: (0, 0, 0), pipeline_mode=pl.Buffered(1)),
            pl.BlockSpec(weight_fwd.shape, lambda r: (0, 0), pipeline_mode=pl.Buffered(1)),
            row(columns, DISP),
        ],
        out_specs=[
            row(C_OUT, columns),
            row(columns, C_OUT),
            row(columns, 2 * DISP),
            row(3 * C_IN, columns),
        ],
        out_shape=[
            jax.ShapeDtypeStruct((rows, C_OUT, columns), BF16),
            jax.ShapeDtypeStruct((rows, columns, C_OUT), BF16),
            jax.ShapeDtypeStruct((rows, columns, 2 * DISP), BF16),
            jax.ShapeDtypeStruct((rows, 3 * C_IN, columns), BF16),
        ],
        scratch_shapes=[pltpu.VMEM((3, 3 * C_IN, columns), BF16)],
        compiler_params=params(40),
        name="own_side",
    )(x_haloed, weight_fwd, cot_haloed)


def pair_kernel(
    off_ref, x_ref, weight_ref, feat_ref, featt_ref, skew_ref, *rest
):
    query_ref, key_ref, tap_ref, taps = rest[-4:]
    r = pl.program_id(0)

    next_row(taps, x_ref, r)
    tap_ref[0] = taps[1]
    feat = conv_row(weight_ref, taps).astype(BF16).astype(F32)
    columns = feat.shape[1]
    blocks = columns // DISP
    wide = columns + 2 * DISP
    move = off_ref[0] + (DISP - 1)
    padded = jnp.concatenate([feat, jnp.zeros((C_OUT, 2 * DISP), F32)], axis=1)
    keyed = pltpu.roll(padded, move, 1)[:, : columns + DISP].astype(BF16)
    scale = 1.0 / math.sqrt(C_OUT)
    heads, tails = [], []
    for b in range(blocks):
        here = slice(b * DISP, (b + 1) * DISP)
        window = keyed[:, b * DISP : (b + 2) * DISP]
        products = jnp.dot(featt_ref[0, here, :], window, preferred_element_type=F32)
        squashed = jnp.tanh(products * scale)
        placed = (
            skew_ref[0, here, :].astype(F32) * (1.0 - squashed * squashed) * scale
        ).astype(BF16)
        query_ref[0, :, here] = lax.dot_general(
            window, placed, (((1,), (1,)), ((), ())), preferred_element_type=F32
        ).astype(BF16)
        grad = jnp.dot(feat_ref[0, :, here], placed, preferred_element_type=F32)
        heads.append(grad[:, :DISP])
        tails.append(grad[:, DISP:])
    tiles = [heads[0]]
    for b in range(1, blocks):
        tiles.append(heads[b] + tails[b - 1])
    tiles += [tails[-1], jnp.zeros_like(tails[-1])]
    key_ref[0] = pltpu.roll(jnp.concatenate(tiles, axis=1), wide - move, 1)[:, :columns].astype(
        BF16
    )


def pair_side(offset, x_part, weight_fwd, feat, featt, skew, base, carried):
    rows, _, columns = feat.shape
    count = x_part.shape[0] - 2
    row = lambda *tail: pl.BlockSpec((1,) + tail, lambda r, off: (r + base,) + (0,) * len(tail))
    whole = lambda a: pl.BlockSpec(
        a.shape, lambda r, off: (0,) * a.ndim, pipeline_mode=pl.Buffered(1)
    )
    operands = [x_part, weight_fwd, feat, featt, skew]
    in_specs = [
        whole(x_part),
        whole(weight_fwd),
        row(C_OUT, columns),
        row(columns, C_OUT),
        row(columns, 2 * DISP),
    ]
    aliases = {}
    if carried is not None:
        for i, buffer in enumerate(carried):
            aliases[1 + len(operands)] = i
            operands.append(buffer)
            in_specs.append(pl.BlockSpec(memory_space=pl.ANY))
    return pl.pallas_call(
        pair_kernel,
        grid_spec=pltpu.PrefetchScalarGridSpec(
            num_scalar_prefetch=1,
            grid=(count,),
            in_specs=in_specs,
            out_specs=[row(C_OUT, columns), row(C_OUT, columns), row(3 * C_IN, columns)],
            scratch_shapes=[pltpu.VMEM((3, 3 * C_IN, columns), BF16)],
        ),
        out_shape=[
            jax.ShapeDtypeStruct((rows, C_OUT, columns), BF16),
            jax.ShapeDtypeStruct((rows, C_OUT, columns), BF16),
            jax.ShapeDtypeStruct((rows, 3 * C_IN, columns), BF16),
        ],
        input_output_aliases=aliases,
        compiler_params=params(32),
        name="pair_side",
    )(offset, *operands)


def back_row(weight_ref, grad_ref, r):
    columns = grad_ref.shape[2]
    patch = grad_ref[pl.ds(r, 3)].reshape(3 * C_OUT, columns)
    taps = jnp.dot(weight_ref[...], patch, preferred_element_type=F32)
    return (
        taps[C_IN : 2 * C_IN]
        + shifted_left(taps[:C_IN])
        + shifted_right(taps[2 * C_IN :])
    )


def key_back_kernel(grad_ref, weight_ref, out_ref):
    out_ref[0] = back_row(weight_ref, grad_ref, pl.program_id(0)).astype(BF16)


def key_back(key, weight_bwd):
    rows, _, columns = key.shape
    return pl.pallas_call(
        key_back_kernel,
        grid=(rows - 2,),
        in_specs=[
            pl.BlockSpec(key.shape, lambda r: (0, 0, 0), pipeline_mode=pl.Buffered(1)),
            pl.BlockSpec(weight_bwd.shape, lambda r: (0, 0), pipeline_mode=pl.Buffered(1)),
        ],
        out_specs=pl.BlockSpec((1, C_IN, columns), lambda r: (r, 0, 0)),
        out_shape=jax.ShapeDtypeStruct((rows - 2, C_IN, columns), BF16),
        compiler_params=params(24),
        name="key_back",
    )(key, weight_bwd)


def image_back_kernel(grad_ref, weight_ref, recv_ref, out_ref):
    out_ref[0] = back_row(weight_ref, grad_ref, pl.program_id(0)) + recv_ref[0].astype(F32)


def image_back(query, weight_bwd, received):
    rows, _, columns = query.shape
    count = rows - 2
    out = pl.pallas_call(
        image_back_kernel,
        grid=(count,),
        in_specs=[
            pl.BlockSpec(query.shape, lambda r: (0, 0, 0), pipeline_mode=pl.Buffered(1)),
            pl.BlockSpec(weight_bwd.shape, lambda r: (0, 0), pipeline_mode=pl.Buffered(1)),
            pl.BlockSpec((1, C_IN, columns), lambda r: (r, 0, 0)),
        ],
        out_specs=pl.BlockSpec((1, C_IN, columns), lambda r: (r, 0, 0)),
        out_shape=jax.ShapeDtypeStruct((count, C_IN, columns), F32),
        compiler_params=params(32),
        name="image_back",
    )(query, weight_bwd, received)
    return jnp.transpose(out, (1, 0, 2))


def weight_kernel(query_ref, key_ref, own_ref, partner_ref, out_ref, acc):
    r = pl.program_id(0)
    columns = query_ref.shape[2]
    contract = (((1,), (1,)), ((), ()))
    own = own_ref[pl.ds(r, 3)].reshape(9 * C_IN, columns)
    partner = partner_ref[pl.ds(r, 3)].reshape(9 * C_IN, columns)
    term = lax.dot_general(
        query_ref[0], own, contract, preferred_element_type=F32
    ) + lax.dot_general(key_ref[0], partner, contract, preferred_element_type=F32)

    @pl.when(r == 0)
    def _():
        acc[...] = term

    @pl.when(r > 0)
    def _():
        acc[...] += term

    @pl.when(r == pl.num_programs(0) - 1)
    def _():
        for tap in range(9):
            out_ref[tap] = acc[:, tap * C_IN : (tap + 1) * C_IN].astype(BF16)


def weight_term(query, key, own_taps, partner_taps):
    rows, _, columns = query.shape
    inner = pl.BlockSpec((1, C_OUT, columns), lambda r: (r + 1, 0, 0))
    taps = pl.BlockSpec(own_taps.shape, lambda r: (0, 0, 0), pipeline_mode=pl.Buffered(1))
    return pl.pallas_call(
        weight_kernel,
        grid=(rows - 2,),
        in_specs=[inner, inner, taps, taps],
        out_specs=pl.BlockSpec((9, C_OUT, C_IN), lambda r: (0, 0, 0)),
        out_shape=jax.ShapeDtypeStruct((9, C_OUT, C_IN), BF16),
        scratch_shapes=[pltpu.VMEM((C_OUT, 9 * C_IN), F32)],
        compiler_params=params(40),
        name="weight_term",
    )(query, key, own_taps, partner_taps)


def passed_along(x, axis, by):
    size = lax.axis_size(axis)
    return lax.ppermute(x, axis, [(i, (i + by) % size) for i in range(size)])


def shifted_bands(x, by):
    size = lax.axis_size("band")
    return lax.ppermute(
        x, "band", [(i, i + by) for i in range(size) if 0 <= i + by < size]
    )


def lookup(table, position):
    places = jnp.arange(table.shape[0], dtype=jnp.int32)
    return jnp.sum(jnp.where(places == position, table, 0), dtype=jnp.int32)


def summed_everywhere(term):
    axes = ("cam", "band")
    count = lax.axis_size("cam") * lax.axis_size("band")
    pieces = term.reshape(count, -1, C_IN)
    mine = lax.all_to_all(pieces, axes, split_axis=0, concat_axis=0, tiled=True)
    piece = jnp.sum(mine.astype(F32), axis=0, keepdims=True).astype(BF16)
    spread = jnp.broadcast_to(piece, pieces.shape)
    return lax.all_to_all(spread, axes, split_axis=0, concat_axis=0, tiled=True)


def per_device(images, weight, offsets, cotangent):
    image = jnp.transpose(images[0], (1, 0, 2))
    cot = cotangent[0]
    rows = image.shape[0]
    columns = image.shape[2]
    part = (rows - 4) // 2
    edges = jnp.concatenate([image[:2], image[-2:]], axis=0)
    partner_edges = passed_along(edges, "cam", -1)
    upper = jnp.concatenate([image[-2:], cot[-1].T[None]], axis=0)
    lower = jnp.concatenate([image[:2], cot[0].T[None]], axis=0)
    low = shifted_bands(upper, 1)
    high = shifted_bands(lower, -1)
    first = passed_along(image[2 : 2 + part], "cam", -1)
    second = passed_along(image[2 + part : 2 + 2 * part], "cam", -1)
    partner_low = shifted_bands(partner_edges[2:], 1)
    partner_high = shifted_bands(partner_edges[:2], -1)

    offset = lookup(offsets, lax.axis_index("cam")).reshape(1)
    weight_fwd = jnp.transpose(weight, (2, 0, 1, 3)).reshape(C_OUT, 9 * C_IN)
    weight_bwd = jnp.transpose(weight[::-1], (1, 3, 0, 2)).reshape(3 * C_IN, 3 * C_OUT)

    haloed = jnp.concatenate([low[:2], image, high[:2]], axis=0)
    cot_haloed = jnp.concatenate([low[2].T[None], cot, high[2].T[None]], axis=0)
    feat, featt, skew, own_taps = own_side(haloed, weight_fwd, cot_haloed)

    top = jnp.concatenate([partner_low, partner_edges[:2], first], axis=0)
    bottom = jnp.concatenate([first[-2:], second, partner_edges[2:], partner_high], axis=0)
    carried = pair_side(offset, top, weight_fwd, feat, featt, skew, 0, None)
    query, key, partner_taps = pair_side(
        offset, bottom, weight_fwd, feat, featt, skew, top.shape[0] - 2, carried
    )
    received = passed_along(key_back(key, weight_bwd), "cam", 1)
    term = weight_term(query, key, own_taps, partner_taps)
    total = summed_everywhere(term)
    normalizer = 1.0 / math.sqrt(lax.axis_size("cam") * lax.axis_size("band") * rows * columns)
    weight_grad = total.astype(F32).reshape(weight.shape) * normalizer
    image_grad = image_back(query, weight_bwd, received)
    return (image_grad[None], weight_grad)


def solution(mesh):
    in_specs = (P("cam", None, "band", None), P(), P(), P("cam", "band", None, None))
    out_specs = (P("cam", None, "band", None), P())
    return jax.shard_map(
        per_device, mesh=mesh, in_specs=in_specs, out_specs=out_specs, check_vma=False
    )
```

profile of v0, /device:TPU:1, one launch (start us, length us, event | category | flops | bytes accessed | tf_op | source)
XLA Modules:
  0.0 260.1 jit_solution(14513318478453681341)
XLA Ops:
  0.6 2.8 %copy.32 = bf16[1,128,16,512]{3,1,2,0:T(8,128)(2,1)S(1)} copy(bf16[1,128,16,512]{3,2,1,0:T(8,128)(2,1)} %param.4) | data formatting | bytes 4194304 | tf_op args[0]
  3.4 1.0 fusion.1
  4.4 0.1 copy.28
  4.5 0.8 pad_maximum_fusion.5
  5.3 6.9 %collective-permute-start.4 = (bf16[3,128,512]{2,1,0:T(8,128)(2,1)}, bf16[3,128,512]{2,1,0:T(8,128)(2,1)}, u32[]{:S(2)}, u32[]{:S(2)}) collective-permute-start(bf16[3,128,512]{2,1,0:T(8,128)(2,1)} %pad_maximum_fusion.5), channel_id=1, source_target_pairs={{0,1},{1,2},{2,3},{4,5},{5,6},{6,7},{8,9},{9,10},{10,11},{12,13},{... | collective-permute-start | bytes 1179656 | tf_op jit(solution)/shard_map/ppermute | solution.py:297
  12.2 0.1 copy.29
  12.3 0.8 pad_maximum_fusion.6
  13.1 2.0 collective-permute-start.5
  15.2 0.8 pad_maximum_fusion.4
  16.0 5.4 %collective-permute-start.2 = (bf16[4,128,512]{2,1,0:T(8,128)(2,1)}, bf16[4,128,512]{2,1,0:T(8,128)(2,1)}, u32[]{:S(2)}, u32[]{:S(2)}) collective-permute-start(bf16[4,128,512]{2,1,0:T(8,128)(2,1)} %pad_maximum_fusion.4), channel_id=1, source_target_pairs={{0,124},{4,0},{8,4},{12,8},{16,12},{20,16},{24,20},{28,24},{32,28}... | collective-permute-start | bytes 1572872 | tf_op jit(solution)/shard_map/ppermute | solution.py:292
  21.4 1.2 fusion.2
  22.6 0.5 collective-permute-start
  23.1 0.2 collective-permute-start.1
  23.3 0.9 reverse_bitcast_fusion
  24.1 1.1 copy.18
  25.2 1.4 copy.25.weight_ref
  26.6 2.2 copy.26
  28.8 1.2 copy.30
  30.1 0.7 fusion
  30.7 0.9 slice_bitcast_fusion.1
  31.7 0.9 slice_bitcast_fusion
  32.6 0.7 copy.21
  33.3 0.8 copy.22
  34.1 1.0 slice.65
  35.1 1.0 slice.66
  36.0 1.1 fusion.4
  37.1 6.7 %collective-permute-start.6 = (bf16[2,128,512]{2,1,0:T(8,128)(2,1)S(1)}, bf16[2,128,512]{2,1,0:T(8,128)(2,1)S(1)}, u32[]{:S(2)}, u32[]{:S(2)}) collective-permute-start(bf16[2,128,512]{2,1,0:T(8,128)(2,1)S(1)} %get-tuple-element.32), channel_id=1, source_target_pairs={{0,1},{1,2},{2,3},{4,5},{5,6},{6,7},{8,9},{9,10},{10,11},{12,13},{... | collective-permute-start | bytes 786440 | tf_op jit(solution)/shard_map/ppermute | solution.py:297
  43.9 0.3 pad_maximum_fusion.x_ref
  44.2 1.9 collective-permute-start.3
  46.2 0.3 pad_maximum_fusion.1.cot_ref
  46.5 15.9 %own_side.1 = (bf16[18,256,512]{2,1,0:T(8,128)(2,1)S(1)}, bf16[18,512,256]{2,1,0:T(8,128)(2,1)}, bf16[18,512,256]{2,1,0:T(8,128)(2,1)}, bf16[18,384,512]{2,1,0:T(8,128)(2,1)}) custom-call(bf16[20,128,512]{2,1,0:T(8,128)(2,1)S(1)} %pad_maximum_fusion.x_ref, bf16[256,1152]{1,0:T(8,128)(2,1)S(1)} %copy.25.weight_ref, ...), custom_call_target="tpu_custom_call" | custom-call | tf_op jit(solution)/shard_map/own_side/pallas_call | solution.py:89
  62.3 1.3 pad_maximum_fusion.3.x_ref
  63.6 2.3 copy-done.2
  65.9 17.8 %pair_side.2 = (bf16[18,256,512]{2,1,0:T(8,128)(2,1)S(1)}, bf16[18,256,512]{2,1,0:T(8,128)(2,1)S(1)}, bf16[18,384,512]{2,1,0:T(8,128)(2,1)}) custom-call(s32[1]{0:T(128)} %bitcast.off_ref, bf16[10,128,512]{2,1,0:T(8,128)(2,1)S(1)} %pad_maximum_fusion.3.x_ref, bf16[256,1152]{1,0:T(8,128)(2,1)S(1)} %copy.25.weight_ref, ...), custom_call_target="tpu_custom_call" | custom-call | tf_op jit(solution)/shard_map/pair_side/pallas_call | solution.py:176
  83.8 1.0 slice.59
  84.8 1.4 pad_maximum_fusion.2.x_ref
  86.1 21.8 %pair_side.3 = (bf16[18,256,512]{2,1,0:T(8,128)(2,1)S(1)}, bf16[18,256,512]{2,1,0:T(8,128)(2,1)S(1)}, bf16[18,384,512]{2,1,0:T(8,128)(2,1)}) custom-call(s32[1]{0:T(128)} %bitcast.off_ref, bf16[12,128,512]{2,1,0:T(8,128)(2,1)S(1)} %pad_maximum_fusion.2.x_ref, ...), custom_call_target="tpu_custom_call", output_to_operand_aliasing={{0}: (6, {}), {1}: (7, {}), {2}: (8, {})} | custom-call | tf_op jit(solution)/shard_map/pair_side/pallas_call | solution.py:176
  107.9 10.9 %key_back.1 = bf16[16,128,512]{2,1,0:T(8,128)(2,1)} custom-call(bf16[18,256,512]{2,1,0:T(8,128)(2,1)S(1)} %get-tuple-element.19.grad_ref.key_ref, bf16[384,768]{1,0:T(8,128)(2,1)S(1)} %bitcast.41), custom_call_target="tpu_custom_call" | custom-call | tf_op jit(solution)/shard_map/key_back/pallas_call | solution.py:213
  118.8 1.3 collective-permute-start.7
  120.0 21.0 %weight_term.1 = bf16[9,256,128]{2,1,0:T(8,128)(2,1)S(1)} custom-call(bf16[18,256,512]{2,1,0:T(8,128)(2,1)S(1)} %get-tuple-element.18.grad_ref.query_ref, bf16[18,256,512]{2,1,0:T(8,128)(2,1)S(1)} %get-tuple-element.19.grad_ref.key_ref, bf16[18,384,512]{2,1,0:T(8,128)(2,1)} %get-tuple-element.20.own_ref, bf16[18,384,512]{2,1,0:T(8,128)(2,1)} %get-tuple-element.21.partner_ref), custom_call_target="tpu_custom_call" | custom-call | tf_op jit(solution)/shard_map/weight_term/pallas_call | solution.py:278
  141.1 0.2 reshape.30
  141.3 75.5 %all_to_all.10 = bf16[128,18,128]{2,1,0:T(8,128)(2,1)S(1)} all-to-all(bf16[128,18,128]{2,1,0:T(8,128)(2,1)S(1)} %reshape.30), channel_id=1, replica_groups=mesh['cam'=32,'band'=4] {'cam','band'}, dimensions={0} | all-to-all | bytes 1179648 | tf_op jit(solution)/shard_map/all_to_all | solution.py:311
  216.8 0.2 reduce_sum.22
  217.1 22.4 %all_to_all.11 = bf16[128,18,128]{2,1,0:T(8,128)(2,1)S(1)} all-to-all(bf16[128,18,128]{2,1,0:T(8,128)(2,1)S(1)} %broadcast_in_dim.31), channel_id=1, replica_groups=mesh['cam'=32,'band'=4] {'cam','band'}, dimensions={0} | all-to-all | bytes 1179648 | tf_op jit(solution)/shard_map/all_to_all | solution.py:314
  239.6 1.1 mul.11
  240.7 2.3 copy-done.1
  243.0 12.6 %image_back.1 = f32[16,128,512]{2,1,0:T(8,128)S(1)} custom-call(bf16[18,256,512]{2,1,0:T(8,128)(2,1)S(1)} %copy-done.1, bf16[384,768]{1,0:T(8,128)(2,1)S(1)} %bitcast.42, bf16[16,128,512]{2,1,0:T(8,128)(2,1)} %collective-permute-done.7.recv_ref), custom_call_target="tpu_custom_call" | custom-call | tf_op jit(solution)/shard_map/image_back/pallas_call | solution.py:234
  255.6 4.4 %copy.27 = f32[1,128,16,512]{3,2,1,0:T(8,128)} copy(f32[1,128,16,512]{3,1,2,0:T(8,128)S(1)} %bitcast.40) | data formatting | bytes 8388608
  (25 shorter events, 0.3 us)
Async XLA Ops:
  5.3 25.4 %collective-permute-start.4 = (bf16[3,128,512]{2,1,0:T(8,128)(2,1)}, bf16[3,128,512]{2,1,0:T(8,128)(2,1)}, u32[]{:S(2)}, u32[]{:S(2)}) collective-permute-start(bf16[3,128,512]{2,1,0:T(8,128)(2,1)} %pad_maximum_fusion.5), channel_id=1, source_target_pairs={{0,1},{1,2},{2,3},{4,5},{5,6},{6,7},{8,9},{9,10},{10,11},{12,13},{... | collective-permute-start | bytes 1179656 | tf_op jit(solution)/shard_map/ppermute | solution.py:297
  13.1 10.1 %copy-start.4 = (bf16[3,3,256,128]{3,2,1,0:T(8,128)(2,1)S(1)}, bf16[3,3,256,128]{3,2,1,0:T(8,128)(2,1)}, u32[]{:S(2)}) copy-start(bf16[3,3,256,128]{3,2,1,0:T(8,128)(2,1)} %param.5) | copy-start | bytes 1769476
  13.1 18.5 %collective-permute-start.5 = (bf16[3,128,512]{2,1,0:T(8,128)(2,1)}, bf16[3,128,512]{2,1,0:T(8,128)(2,1)}, u32[]{:S(2)}, u32[]{:S(2)}) collective-permute-start(bf16[3,128,512]{2,1,0:T(8,128)(2,1)} %pad_maximum_fusion.6), channel_id=1, source_target_pairs={{1,0},{2,1},{3,2},{5,4},{6,5},{7,6},{9,8},{10,9},{11,10},{13,12},{... | collective-permute-start | bytes 1179656 | tf_op jit(solution)/shard_map/ppermute | solution.py:297
  16.0 20.0 %collective-permute-start.2 = (bf16[4,128,512]{2,1,0:T(8,128)(2,1)}, bf16[4,128,512]{2,1,0:T(8,128)(2,1)}, u32[]{:S(2)}, u32[]{:S(2)}) collective-permute-start(bf16[4,128,512]{2,1,0:T(8,128)(2,1)} %pad_maximum_fusion.4), channel_id=1, source_target_pairs={{0,124},{4,0},{8,4},{12,8},{16,12},{20,16},{24,20},{28,24},{32,28}... | collective-permute-start | bytes 1572872 | tf_op jit(solution)/shard_map/ppermute | solution.py:292
  22.6 39.7 %collective-permute-start = (bf16[6,128,512]{2,1,0:T(8,128)(2,1)}, bf16[6,128,512]{2,1,0:T(8,128)(2,1)}, u32[]{:S(2)}, u32[]{:S(2)}) collective-permute-start(bf16[6,128,512]{2,1,0:T(8,128)(2,1)} %get-tuple-element.28), channel_id=1, source_target_pairs={{0,124},{4,0},{8,4},{12,8},{16,12},{20,16},{24,20},{28,24},{32,28}... | collective-permute-start | bytes 2359304 | tf_op jit(solution)/shard_map/ppermute | solution.py:292
  23.1 61.6 %collective-permute-start.1 = (bf16[6,128,512]{2,1,0:T(8,128)(2,1)}, bf16[6,128,512]{2,1,0:T(8,128)(2,1)}, u32[]{:S(2)}, u32[]{:S(2)}) collective-permute-start(bf16[6,128,512]{2,1,0:T(8,128)(2,1)} %get-tuple-element.29), channel_id=1, source_target_pairs={{0,124},{4,0},{8,4},{12,8},{16,12},{20,16},{24,20},{28,24},{32,28}... | collective-permute-start | bytes 2359304 | tf_op jit(solution)/shard_map/ppermute | solution.py:292
  25.2 4.8 %copy-start.7 = (s32[32]{0:T(128)S(1)}, s32[32]{0:T(128)}, u32[]{:S(2)}) copy-start(s32[32]{0:T(128)} %param.6) | copy-start | bytes 388
  37.1 9.0 %copy-start.3 = (bf16[1,16,512,128]{3,2,1,0:T(8,128)(2,1)S(1)}, bf16[1,16,512,128]{3,2,1,0:T(8,128)(2,1)}, u32[]{:S(2)}) copy-start(bf16[1,16,512,128]{3,2,1,0:T(8,128)(2,1)} %param.7) | copy-start | bytes 6291460
  37.1 9.0 %copy-start.5 = (bf16[1,512,128]{2,1,0:T(8,128)(2,1)S(1)}, bf16[1,512,128]{2,1,0:T(8,128)(2,1)}, u32[]{:S(2)}) copy-start(bf16[1,512,128]{2,1,0:T(8,128)(2,1)} %copy.21) | copy-start | bytes 393220
  37.1 9.0 %copy-start.6 = (bf16[1,512,128]{2,1,0:T(8,128)(2,1)S(1)}, bf16[1,512,128]{2,1,0:T(8,128)(2,1)}, u32[]{:S(2)}) copy-start(bf16[1,512,128]{2,1,0:T(8,128)(2,1)} %copy.22) | copy-start | bytes 393220
  37.1 25.2 %collective-permute-start.6 = (bf16[2,128,512]{2,1,0:T(8,128)(2,1)S(1)}, bf16[2,128,512]{2,1,0:T(8,128)(2,1)S(1)}, u32[]{:S(2)}, u32[]{:S(2)}) collective-permute-start(bf16[2,128,512]{2,1,0:T(8,128)(2,1)S(1)} %get-tuple-element.32), channel_id=1, source_target_pairs={{0,1},{1,2},{2,3},{4,5},{5,6},{6,7},{8,9},{9,10},{10,11},{12,13},{... | collective-permute-start | bytes 786440 | tf_op jit(solution)/shard_map/ppermute | solution.py:297
  44.2 40.5 %collective-permute-start.3 = (bf16[2,128,512]{2,1,0:T(8,128)(2,1)S(1)}, bf16[2,128,512]{2,1,0:T(8,128)(2,1)S(1)}, u32[]{:S(2)}, u32[]{:S(2)}) collective-permute-start(bf16[2,128,512]{2,1,0:T(8,128)(2,1)S(1)} %get-tuple-element.33), channel_id=1, source_target_pairs={{1,0},{2,1},{3,2},{5,4},{6,5},{7,6},{9,8},{10,9},{11,10},{13,12},{... | collective-permute-start | bytes 786440 | tf_op jit(solution)/shard_map/ppermute | solution.py:297
  63.6 2.3 copy-start.2
  107.9 12.1 %copy-start = (bf16[18,256,512]{2,1,0:T(8,128)(2,1)}, bf16[18,256,512]{2,1,0:T(8,128)(2,1)S(1)}, u32[]{:S(2)}) copy-start(bf16[18,256,512]{2,1,0:T(8,128)(2,1)S(1)} %get-tuple-element.18.grad_ref.query_ref) | copy-start | bytes 14155780
  118.8 121.9 %collective-permute-start.7 = (bf16[16,128,512]{2,1,0:T(8,128)(2,1)}, bf16[16,128,512]{2,1,0:T(8,128)(2,1)}, u32[]{:S(2)}, u32[]{:S(2)}) collective-permute-start(bf16[16,128,512]{2,1,0:T(8,128)(2,1)} %key_back.1), channel_id=1, source_target_pairs={{0,4},{4,8},{8,12},{12,16},{16,20},{20,24},{24,28},{28,32},{32,36}... | collective-permute-start | bytes 6291464 | tf_op jit(solution)/shard_map/ppermute | solution.py:292
  240.7 2.3 copy-start.1
where the time goes:
time: 261 us; the launch traced here: 260 us
  Pallas kernels  99.9 us (38%)
  blocking collectives  97.9 us (38%)
  local copies, waits for them, and re-layouts  29.8 us (11%)
  starting transfers between devices  24.9 us (10%)
  other arithmetic  6.59 us (3%)
    all_to_all x1, blocking collectives, summed_everywhere(): mine = lax.all_to_all(pieces, axes, split_axis=0, concat_axis=0, tiled=True)  75.5 us
    pallas_call x2, Pallas kernels, pair_side(): pl.pallas_call(pair_kernel, grid_spec=pltpu.PrefetchScalarGridSpec(num_sc...  39.6 us
    all_to_all x1, blocking collectives, summed_everywhere(): return lax.all_to_all(spread, axes, split_axis=0, concat_axis=0, tiled=True)  22.4 us
    pallas_call x1, Pallas kernels, weight_term(): pl.pallas_call(weight_kernel, grid=(rows - 2,), in_specs=[inner, inner, t...  21 us
    ppermute x4, starting transfers between devices, shifted_bands(): lax.ppermute(x, 'band', [(i, i + by) for i in range(size) if 0 <= i + by...  17.6 us
    pallas_call x1, Pallas kernels, own_side(): pl.pallas_call(own_kernel, grid=(rows,), in_specs=[pl.BlockSpec(x_haloed....  15.9 us
    unnamed x22, local copies, waits for them, and re-layouts  14.4 us
    pallas_call x1, Pallas kernels, image_back(): pl.pallas_call(image_back_kernel, grid=(count,), in_specs=[pl.BlockSpec(q...  12.6 us
  transfers between devices with their start and end apart: 8, of which 0 were waited for; matrix products, arithmetic and copies ran while one was open for 8% of the time, Pallas kernels for 21%

commit v1 on v0

v1 whole, which is shorter than its diff:
```python
import math

import jax
import jax.numpy as jnp
from jax import lax
from jax.experimental import pallas as pl
from jax.experimental.pallas import tpu as pltpu
from jax.sharding import PartitionSpec as P

C_IN = 128
C_OUT = 256
DISP = 128
F32 = jnp.float32
BF16 = jnp.bfloat16
MIB = 1024 * 1024


def params(limit_mib=60):
    return pltpu.CompilerParams(
        dimension_semantics=("arbitrary",), vmem_limit_bytes=limit_mib * MIB
    )


def without_lane(tile, place):
    lane = lax.broadcasted_iota(jnp.int32, tile.shape, 1)
    return jnp.where(lane == place, 0.0, tile)


def shifted_right(x):
    moved = pltpu.roll(x, 1, 1)
    return jnp.concatenate([without_lane(moved[:, :DISP], 0), moved[:, DISP:]], axis=1)


def shifted_left(x):
    width = x.shape[1]
    moved = pltpu.roll(x, width - 1, 1)
    return jnp.concatenate(
        [moved[:, : width - DISP], without_lane(moved[:, width - DISP :], DISP - 1)], axis=1
    )


def put_taps(taps_ref, place, row):
    wide = row.astype(F32)
    taps_ref[place, :C_IN, :] = shifted_right(wide).astype(BF16)
    taps_ref[place, C_IN : 2 * C_IN, :] = row
    taps_ref[place, 2 * C_IN :, :] = shifted_left(wide).astype(BF16)


def row_at(pieces, refs, t):
    for (start, count), ref in zip(pieces, refs):
        if t < count:
            return ref[start + t]
        t -= count


def fetch_row(pieces, refs, row_ref, t):
    first = 0
    for (start, count), ref in zip(pieces, refs):
        low, high = first, first + count

        @pl.when((t >= low) & (t < high))
        def _(ref=ref, start=start, low=low):
            row_ref[...] = ref[t - low + start]

        first = high


def next_row(pieces, refs, taps_ref, row_ref, r):
    total = sum(count for _, count in pieces)

    @pl.when(r == 0)
    def _():
        put_taps(taps_ref, 1, row_at(pieces, refs, 0))
        put_taps(taps_ref, 2, row_at(pieces, refs, 1))

    fetch_row(pieces, refs, row_ref, jnp.minimum(r + 2, total - 1))
    taps_ref[0] = taps_ref[1]
    taps_ref[1] = taps_ref[2]
    put_taps(taps_ref, 2, row_ref[...])


def conv_row(weight_ref, taps_ref):
    patch = taps_ref[...].reshape(9 * C_IN, taps_ref.shape[2])
    return jnp.dot(weight_ref[...], patch, preferred_element_type=F32)


def whole(a):
    return pl.BlockSpec(a.shape, lambda *_: (0,) * a.ndim, pipeline_mode=pl.Buffered(1))


def own_kernel(pieces, carried, *refs):
    count = len(pieces)
    x_refs = refs[:count]
    weight_ref, cot_ref = refs[count : count + 2]
    feat_ref, featt_ref, skew_ref, tap_ref, taps, row = refs[count + 2 + carried :]
    r = pl.program_id(0)
    next_row(pieces, x_refs, taps, row, r)
    feat = conv_row(weight_ref, taps)
    feat_ref[0] = feat.astype(BF16)
    featt_ref[0] = feat.T.astype(BF16)
    tap_ref[0] = taps[1]
    rows = lax.broadcasted_iota(jnp.int32, (DISP, DISP), 0)
    cols = lax.broadcasted_iota(jnp.int32, (DISP, DISP), 1)
    exchange = jnp.where(rows + cols == DISP - 1, 1.0, 0.0).astype(BF16)
    flipped = jnp.dot(cot_ref[0], exchange, preferred_element_type=F32)
    blocks = flipped.shape[0] // DISP
    for b in range(blocks):
        part = flipped[b * DISP : (b + 1) * DISP]
        wide = jnp.concatenate([part, jnp.zeros_like(part)], axis=1)
        skew_ref[0, b * DISP : (b + 1) * DISP] = pltpu.roll(
            wide, 1, 1, stride=1, stride_axis=0
        ).astype(BF16)


def own_side(pieces, parts, weight_fwd, cot, rows, place, cot_place, carried):
    _, columns, _ = cot.shape
    count = sum(n for _, n in pieces) - 2
    row = lambda *tail: pl.BlockSpec((1,) + tail, lambda r: (place(r),) + (0,) * len(tail))
    operands = [*parts, weight_fwd, cot]
    in_specs = [
        *[whole(part) for part in parts],
        whole(weight_fwd),
        pl.BlockSpec((1, columns, DISP), lambda r: (cot_place(r), 0, 0)),
    ]
    aliases = {}
    for i, buffer in enumerate(carried):
        aliases[len(operands)] = i
        operands.append(buffer)
        in_specs.append(pl.BlockSpec(memory_space=pl.ANY))
    return pl.pallas_call(
        lambda *refs: own_kernel(pieces, len(carried), *refs),
        grid=(count,),
        in_specs=in_specs,
        out_specs=[
            row(C_OUT, columns),
            row(columns, C_OUT),
            row(columns, 2 * DISP),
            row(3 * C_IN, columns),
        ],
        out_shape=[
            jax.ShapeDtypeStruct((rows, C_OUT, columns), BF16),
            jax.ShapeDtypeStruct((rows, columns, C_OUT), BF16),
            jax.ShapeDtypeStruct((rows, columns, 2 * DISP), BF16),
            jax.ShapeDtypeStruct((rows, 3 * C_IN, columns), BF16),
        ],
        input_output_aliases=aliases,
        scratch_shapes=[
            pltpu.VMEM((3, 3 * C_IN, columns), BF16),
            pltpu.VMEM((C_IN, columns), BF16),
        ],
        compiler_params=params(),
        name="own_side",
    )(*operands)


def pair_kernel(pieces, carried, off_ref, *refs):
    count = len(pieces)
    x_refs = refs[:count]
    weight_ref, feat_ref, featt_ref, skew_ref = refs[count : count + 4]
    query_ref, key_ref, tap_ref, taps, row, keys = refs[count + 4 + carried :]
    r = pl.program_id(0)
    blocks = feat_ref.shape[2] // DISP
    columns = blocks * DISP
    offset = off_ref[0]
    scale = 1.0 / math.sqrt(C_OUT)
    keyed = keys[...]
    next_row(pieces, x_refs, taps, row, r)
    feat = conv_row(weight_ref, taps).astype(BF16).astype(F32)

    heads, tails = [], []
    for b in range(blocks):
        here = slice(b * DISP, (b + 1) * DISP)
        window = keyed[:, b * DISP : (b + 2) * DISP]
        products = jnp.dot(featt_ref[0, here, :], window, preferred_element_type=F32)
        squashed = jnp.tanh(products * scale)
        placed = (
            skew_ref[0, here, :].astype(F32) * (1.0 - squashed * squashed) * scale
        ).astype(BF16)
        query_ref[0, :, here] = lax.dot_general(
            window, placed, (((1,), (1,)), ((), ())), preferred_element_type=F32
        ).astype(BF16)
        grad = jnp.dot(feat_ref[0, :, here], placed, preferred_element_type=F32)
        heads.append(grad[:, :DISP])
        tails.append(grad[:, DISP:])
    back = jnp.where(offset == 0, 0, DISP - offset)
    lane = lax.broadcasted_iota(jnp.int32, (C_OUT, DISP), 1)
    moved = []
    for b in range(blocks):
        tile = tails[b] if b == blocks - 1 else tails[b] + heads[b + 1]
        moved.append(pltpu.roll(tile, back, 1))
    moved.append(jnp.zeros_like(moved[0]))
    for b in range(blocks):
        key_ref[0, :, b * DISP : (b + 1) * DISP] = jnp.where(
            lane < DISP - offset, moved[b], moved[b + 1]
        ).astype(BF16)
    tap_ref[0] = taps[0]

    empty = jnp.zeros((C_OUT, DISP), F32)
    moved = [empty]
    for b in range(blocks):
        moved.append(pltpu.roll(feat[:, b * DISP : (b + 1) * DISP], offset, 1))
    keys[:, :DISP] = empty.astype(BF16)
    for b in range(blocks):
        keys[:, (b + 1) * DISP : (b + 2) * DISP] = jnp.where(
            lane >= offset, moved[b + 1], moved[b]
        ).astype(BF16)


def pair_side(offset, pieces, parts, weight_fwd, feat, featt, skew, place, carried):
    rows, _, columns = feat.shape
    count = sum(n for _, n in pieces) - 2
    row = lambda *tail: pl.BlockSpec(
        (1,) + tail, lambda r, off: (place(jnp.maximum(r - 1, 0)),) + (0,) * len(tail)
    )
    operands = [*parts, weight_fwd, feat, featt, skew]
    in_specs = [
        *[whole(part) for part in parts],
        whole(weight_fwd),
        row(C_OUT, columns),
        row(columns, C_OUT),
        row(columns, 2 * DISP),
    ]
    aliases = {}
    for i, buffer in enumerate(carried):
        aliases[1 + len(operands)] = i
        operands.append(buffer)
        in_specs.append(pl.BlockSpec(memory_space=pl.ANY))
    return pl.pallas_call(
        lambda *refs: pair_kernel(pieces, len(carried), *refs),
        grid_spec=pltpu.PrefetchScalarGridSpec(
            num_scalar_prefetch=1,
            grid=(count + 1,),
            in_specs=in_specs,
            out_specs=[row(C_OUT, columns), row(C_OUT, columns), row(3 * C_IN, columns)],
            scratch_shapes=[
                pltpu.VMEM((3, 3 * C_IN, columns), BF16),
                pltpu.VMEM((C_IN, columns), BF16),
                pltpu.VMEM((C_OUT, columns + DISP), BF16),
            ],
        ),
        out_shape=[
            jax.ShapeDtypeStruct((rows, C_OUT, columns), BF16),
            jax.ShapeDtypeStruct((rows, C_OUT, columns), BF16),
            jax.ShapeDtypeStruct((rows, 3 * C_IN, columns), BF16),
        ],
        input_output_aliases=aliases,
        compiler_params=params(),
        name="pair_side",
    )(offset, *operands)


def back_row(weight_ref, grad_ref, r):
    taps = jnp.dot(weight_ref[:, 2 * C_OUT :], grad_ref[r], preferred_element_type=F32)
    taps += jnp.dot(
        weight_ref[:, C_OUT : 2 * C_OUT], grad_ref[r + 1], preferred_element_type=F32
    )
    taps += jnp.dot(weight_ref[:, :C_OUT], grad_ref[r + 2], preferred_element_type=F32)
    return (
        taps[C_IN : 2 * C_IN] + shifted_left(taps[:C_IN]) + shifted_right(taps[2 * C_IN :])
    )


GROUP = 4


def window(depth, columns, first=0, step=GROUP):
    return pl.BlockSpec(
        (pl.Element(GROUP + 2), pl.Element(depth), pl.Element(columns)),
        lambda s: (s * step + first, 0, 0),
    )


def key_back_kernel(grad_ref, weight_ref, out_ref):
    for r in range(GROUP):
        out_ref[r] = back_row(weight_ref, grad_ref, r).astype(BF16)


def key_back(key, weight_bwd, first, step, groups):
    columns = key.shape[2]
    return pl.pallas_call(
        key_back_kernel,
        grid=(groups,),
        in_specs=[window(C_OUT, columns, first, step), whole(weight_bwd)],
        out_specs=pl.BlockSpec((GROUP, C_IN, columns), lambda s: (s, 0, 0)),
        out_shape=jax.ShapeDtypeStruct((groups * GROUP, C_IN, columns), BF16),
        compiler_params=params(),
        name="key_back",
    )(key, weight_bwd)


def image_back_kernel(grad_ref, weight_ref, inner_ref, outer_ref, out_ref):
    s = pl.program_id(0)
    inside = (s > 0) & (s < pl.num_programs(0) - 1)
    for r in range(GROUP):
        out_ref[r] = back_row(weight_ref, grad_ref, r)

    @pl.when(inside)
    def _():
        out_ref[...] += inner_ref[...].astype(F32)

    @pl.when(jnp.logical_not(inside))
    def _():
        out_ref[...] += outer_ref[...].astype(F32)


def image_back(query, weight_bwd, inner, outer):
    rows, _, columns = query.shape
    count = rows - 2
    groups = count // GROUP
    block = (GROUP, C_IN, columns)
    out = pl.pallas_call(
        image_back_kernel,
        grid=(groups,),
        in_specs=[
            window(C_OUT, columns),
            whole(weight_bwd),
            pl.BlockSpec(block, lambda s: (jnp.clip(s - 1, 0, groups - 3), 0, 0)),
            pl.BlockSpec(block, lambda s: (s // (groups - 1), 0, 0)),
        ],
        out_specs=pl.BlockSpec(block, lambda s: (s, 0, 0)),
        out_shape=jax.ShapeDtypeStruct((count, C_IN, columns), F32),
        compiler_params=params(),
        name="image_back",
    )(query, weight_bwd, inner, outer)
    return jnp.transpose(out, (1, 0, 2))


def weight_kernel(query_ref, key_ref, own_ref, partner_ref, out_ref, acc):
    s = pl.program_id(0)
    columns = query_ref.shape[2]
    contract = (((1,), (1,)), ((), ()))

    @pl.when(s == 0)
    def _():
        acc[...] = jnp.zeros_like(acc)

    term = acc[...]
    for r in range(GROUP):
        own = own_ref[r : r + 3].reshape(9 * C_IN, columns)
        partner = partner_ref[r : r + 3].reshape(9 * C_IN, columns)
        term += lax.dot_general(query_ref[r + 1], own, contract, preferred_element_type=F32)
        term += lax.dot_general(key_ref[r + 1], partner, contract, preferred_element_type=F32)
    acc[...] = term

    @pl.when(s == pl.num_programs(0) - 1)
    def _():
        for tap in range(9):
            out_ref[tap] = acc[:, tap * C_IN : (tap + 1) * C_IN].astype(BF16)


def weight_term(query, key, own_taps, partner_taps):
    rows, _, columns = query.shape
    grads = window(C_OUT, columns)
    taps = window(3 * C_IN, columns)
    return pl.pallas_call(
        weight_kernel,
        grid=((rows - 2) // GROUP,),
        in_specs=[grads, grads, taps, taps],
        out_specs=pl.BlockSpec((9, C_OUT, C_IN), lambda s: (0, 0, 0)),
        out_shape=jax.ShapeDtypeStruct((9, C_OUT, C_IN), BF16),
        scratch_shapes=[pltpu.VMEM((C_OUT, 9 * C_IN), F32)],
        compiler_params=params(),
        name="weight_term",
    )(query, key, own_taps, partner_taps)


def passed_along(x, axis, by):
    size = lax.axis_size(axis)
    return lax.ppermute(x, axis, [(i, (i + by) % size) for i in range(size)])


def shifted_bands(x, by):
    size = lax.axis_size("band")
    return lax.ppermute(
        x, "band", [(i, i + by) for i in range(size) if 0 <= i + by < size]
    )


def diagonal(x, by):
    cams, bands = lax.axis_size("cam"), lax.axis_size("band")
    pairs = [
        ((c + 1) % cams * bands + b - by, c * bands + b)
        for c in range(cams)
        for b in range(bands)
        if 0 <= b - by < bands
    ]
    return lax.ppermute(x, ("cam", "band"), pairs)


def lookup(table, position):
    places = jnp.arange(table.shape[0], dtype=jnp.int32)
    return jnp.sum(jnp.where(places == position, table, 0), dtype=jnp.int32)


def summed_everywhere(term):
    axes = ("cam", "band")
    count = lax.axis_size("cam") * lax.axis_size("band")
    pieces = term.reshape(count, -1, C_IN)
    mine = lax.all_to_all(pieces, axes, split_axis=0, concat_axis=0, tiled=True)
    piece = jnp.sum(mine.astype(F32), axis=0, keepdims=True).astype(BF16)
    spread = jnp.broadcast_to(piece, pieces.shape)
    return lax.all_to_all(spread, axes, split_axis=0, concat_axis=0, tiled=True)


def per_device(images, weight, offsets, cotangent):
    image = jnp.transpose(images[0], (1, 0, 2))
    cot = cotangent[0]
    rows = image.shape[0]
    columns = image.shape[2]
    first, last = image[:2], image[-2:]
    low = shifted_bands(jnp.concatenate([last, cot[-1].T[None]], axis=0), 1)
    high = shifted_bands(jnp.concatenate([first, cot[0].T[None]], axis=0), -1)
    inner = passed_along(image[2:-2], "cam", -1)
    edges = passed_along(jnp.concatenate([first, last], axis=0), "cam", -1)
    partner_low = diagonal(last, 1)
    partner_high = diagonal(first, -1)

    offset = lookup(offsets, lax.axis_index("cam")).reshape(1)
    weight_fwd = jnp.transpose(weight, (2, 0, 1, 3)).reshape(C_OUT, 9 * C_IN)
    weight_bwd = jnp.transpose(weight, (1, 3, 0, 2)).reshape(3 * C_IN, 3 * C_OUT)

    total_rows = rows + 2
    own = own_side(
        ((0, rows),), (image,), weight_fwd, cot, total_rows, lambda r: r + 2, lambda r: r + 1, ()
    )
    carried = pair_side(
        offset, ((0, rows - 4),), (inner,), weight_fwd, *own[:3], lambda t: t + 4, ()
    )
    inner_back = key_back(carried[1], weight_bwd, GROUP, GROUP, rows // GROUP - 2)
    sent_inner = passed_along(inner_back, "cam", 1)
    own, carried, low, high = lax.optimization_barrier((own, carried, low, high))
    cot_ends = jnp.stack([low[2].T, cot[0], cot[-1], high[2].T])
    feat, featt, skew, own_taps = own_side(
        ((0, 2), (0, 2), (rows - 2, 2), (0, 2)),
        (low, image, image, high),
        weight_fwd,
        cot_ends,
        total_rows,
        lambda r: jnp.where(r < 2, r, jnp.maximum(r - 4, 0) + rows),
        lambda r: jnp.where(r < 2, r, jnp.maximum(r - 4, 0) + 2),
        own,
    )
    query, key, partner_taps = pair_side(
        offset,
        ((0, 2), (0, 2), (0, 2), (rows - 6, 2), (2, 2), (0, 2)),
        (partner_low, edges, inner, inner, edges, partner_high),
        weight_fwd,
        feat,
        featt,
        skew,
        lambda t: jnp.where(t < 4, t, jnp.maximum(t - 6, 0) + rows - 2),
        carried,
    )
    outer_back = key_back(key, weight_bwd, 0, rows - GROUP, 2)
    sent_outer = passed_along(outer_back, "cam", 1)
    key, sent_inner, _ = lax.optimization_barrier((key, sent_inner, outer_back))
    term = weight_term(query, key, own_taps, partner_taps)
    term, sent_outer = lax.optimization_barrier((term, sent_outer))
    total = summed_everywhere(term)
    normalizer = 1.0 / math.sqrt(lax.axis_size("cam") * lax.axis_size("band") * rows * columns)
    weight_grad = total.astype(F32).reshape(weight.shape) * normalizer
    query, total = lax.optimization_barrier((query, total))
    image_grad = image_back(query, weight_bwd, sent_inner, sent_outer)
    return (image_grad[None], weight_grad)


def solution(mesh):
    in_specs = (P("cam", None, "band", None), P(), P(), P("cam", "band", None, None))
    out_specs = (P("cam", None, "band", None), P())
    return jax.shard_map(
        per_device, mesh=mesh, in_specs=in_specs, out_specs=out_specs, check_vma=False
    )
```

time: 261 us -> 212 us (0.81)
  blocking collectives: 97.9 us -> 43.2 us
  local copies, waits for them, and re-layouts: 29.8 us -> 20.9 us
  waiting for transfers between devices: 0.02 us -> 8.21 us
  Pallas kernels: 99.9 us -> 107 us
    all_to_all x1, blocking collectives: 75.5 us -> 22.9 us  [summed_everywhere(): mine = lax.all_to_all(pieces, axes, split_axis=0, concat_axis=0, tiled=True)]
    ppermute x0 -> x2, starting transfers between devices: none -> 10.9 us  [diagonal(): return lax.ppermute(x, ('cam', 'band'), pairs)]
    ppermute x4 -> x2, starting transfers between devices: 17.6 us -> 7.95 us  [shifted_bands(): lax.ppermute(x, 'band', [(i, i + by) for i in range(size) if 0 <= i + by...]
    ppermute x4, waiting for transfers between devices: 0.01 us -> 8.2 us  [passed_along(): return lax.ppermute(x, axis, [(i, (i + by) % size) for i in range(size)])]
    pallas_call x6 -> x8, Pallas kernels: 99.9 us -> 107 us  [the longest x2 45.7 us: pair_side(): pl.pallas_call(lambda *refs: pair_kernel(pieces, len(carried), *refs), gr...]
    broadcast_in_dim x4 -> x0, local copies, waits for them, and re-layouts: 3.33 us -> none  [per_device(): cot_haloed = jnp.concatenate([low[2].T[None], cot, high[2].T[None]], axis=0)]
    slice x7 -> x3, local copies, waits for them, and re-layouts: 6.24 us -> 3.12 us  [the longest x1 1.36 us: per_device(): inner = passed_along(image[2:-2], 'cam', -1)]
    unnamed x22 -> x24, local copies, waits for them, and re-layouts: 14.4 us -> 11.5 us
  transfers between devices with their start and end apart: 8 -> 8, of which waited for: 0 -> 1; matrix products, arithmetic and copies ran while one was open for 8% -> 6% of each run, Pallas kernels for 21% -> 46%
where the time goes in v1:
time: 212 us; the launch traced here: 211 us
  Pallas kernels  107 us (50%)
  blocking collectives  43.2 us (20%)
  starting transfers between devices  26 us (12%)
  local copies, waits for them, and re-layouts  20.9 us (10%)
  waiting for transfers between devices  8.21 us (4%)
  other arithmetic  5.34 us (3%)
    pallas_call x2, Pallas kernels, pair_side(): pl.pallas_call(lambda *refs: pair_kernel(pieces, len(carried), *refs), gr...  45.7 us
    pallas_call x2, Pallas kernels, own_side(): pl.pallas_call(lambda *refs: own_kernel(pieces, len(carried), *refs), gri...  24.2 us
    all_to_all x1, blocking collectives, summed_everywhere(): mine = lax.all_to_all(pieces, axes, split_axis=0, concat_axis=0, tiled=True)  22.9 us
    all_to_all x1, blocking collectives, summed_everywhere(): return lax.all_to_all(spread, axes, split_axis=0, concat_axis=0, tiled=True)  20.3 us
    pallas_call x1, Pallas kernels, weight_term(): pl.pallas_call(weight_kernel, grid=((rows - 2) // GROUP,), in_specs=[grad...  16.7 us
    unnamed x24, local copies, waits for them, and re-layouts  11.5 us
    ppermute x2, starting transfers between devices, diagonal(): return lax.ppermute(x, ('cam', 'band'), pairs)  10.9 us
    pallas_call x2, Pallas kernels, key_back(): pl.pallas_call(key_back_kernel, grid=(groups,), in_specs=[window(C_OUT, c...  10.7 us
  transfers between devices with their start and end apart: 8, of which 1 were waited for; matrix products, arithmetic and copies ran while one was open for 6% of the time, Pallas kernels for 46%

profile of v1, /device:TPU:1, one launch (start us, length us, event | category | flops | bytes accessed | tf_op | source)
XLA Modules:
  0.0 211.4 jit_solution(2656220552961615384)
XLA Ops:
  0.6 2.8 %copy.35 = bf16[1,128,16,512]{3,1,2,0:T(8,128)(2,1)S(1)} copy(bf16[1,128,16,512]{3,2,1,0:T(8,128)(2,1)} %param.4) | data formatting | bytes 4194304 | tf_op args[0]
  3.4 0.0 copy-start
  3.4 0.0 copy-start.1
  3.4 1.4 slice.40
  4.8 7.1 %collective-permute-start.2 = (bf16[12,128,512]{2,1,0:T(8,128)(2,1)}, bf16[12,128,512]{2,1,0:T(8,128)(2,1)}, u32[]{:S(2)}, u32[]{:S(2)}) collective-permute-start(bf16[12,128,512]{2,1,0:T(8,128)(2,1)} %slice.40), channel_id=1, source_target_pairs={{0,124},{4,0},{8,4},{12,8},{16,12},{20,16},{24,20},{28,24},{32,28}... | collective-permute-start | bytes 4718600 | tf_op jit(solution)/shard_map/ppermute | solution.py:369
  11.9 1.0 fusion.1
  12.9 0.1 copy.31
  13.0 0.8 fusion.2
  13.8 1.7 pad_maximum_fusion.2
  15.5 6.0 %collective-permute-start.4 = (bf16[3,128,512]{2,1,0:T(8,128)(2,1)}, bf16[3,128,512]{2,1,0:T(8,128)(2,1)}, u32[]{:S(2)}, u32[]{:S(2)}) collective-permute-start(bf16[3,128,512]{2,1,0:T(8,128)(2,1)} %pad_maximum_fusion.2), channel_id=1, source_target_pairs={{0,1},{1,2},{2,3},{4,5},{5,6},{6,7},{8,9},{9,10},{10,11},{12,13},{... | collective-permute-start | bytes 1179656 | tf_op jit(solution)/shard_map/ppermute | solution.py:374
  21.5 0.1 copy.32
  21.7 0.8 pad_maximum_fusion.3
  22.5 1.9 collective-permute-start.5
  24.4 1.8 pad_maximum_fusion
  26.2 4.9 %collective-permute-start = (bf16[2,128,512]{2,1,0:T(8,128)(2,1)}, bf16[2,128,512]{2,1,0:T(8,128)(2,1)}, u32[]{:S(2)}, u32[]{:S(2)}) collective-permute-start(bf16[2,128,512]{2,1,0:T(8,128)(2,1)} %get-tuple-element.65), channel_id=1, source_target_pairs={{4,1},{5,2},{6,3},{8,5},{9,6},{10,7},{12,9},{13,10},{14,11},{16,13... | collective-permute-start | bytes 786440 | tf_op jit(solution)/shard_map/ppermute | solution.py:387
  31.1 0.0 copy-start.8
  31.1 0.2 copy.21
  31.4 1.1 copy.28.refs_1_.refs_2_.refs_4_.refs_7_
  32.5 0.7 copy.29
  33.2 0.9 copy.33
  34.1 15.4 %own_side.2 = (bf16[18,256,512]{2,1,0:T(8,128)(2,1)}, bf16[18,512,256]{2,1,0:T(8,128)(2,1)}, bf16[18,512,256]{2,1,0:T(8,128)(2,1)}, bf16[18,384,512]{2,1,0:T(8,128)(2,1)}) custom-call(bf16[16,128,512]{2,1,0:T(8,128)(2,1)} %bitcast.43, bf16[256,1152]{1,0:T(8,128)(2,1)} %copy.28.refs_1_.refs_2_.refs_4_.refs_7_, bf16[16,512,128]{2,1,0:T(8,128)(2,1)} %bitcast.51), custom_call_target="tpu_custom_call" | custom-call | tf_op jit(solution)/shard_map/own_side/pallas_call | solution.py:130
  49.5 0.7 fusion
  50.2 6.0 %collective-permute-start.3 = (bf16[2,128,512]{2,1,0:T(8,128)(2,1)S(1)}, bf16[2,128,512]{2,1,0:T(8,128)(2,1)S(1)}, u32[]{:S(2)}, u32[]{:S(2)}) collective-permute-start(bf16[2,128,512]{2,1,0:T(8,128)(2,1)S(1)} %get-tuple-element.64), channel_id=1, source_target_pairs={{5,0},{6,1},{7,2},{9,4},{10,5},{11,6},{13,8},{14,9},{15,10},{17,12... | collective-permute-start | bytes 786440 | tf_op jit(solution)/shard_map/ppermute | solution.py:387
  56.3 22.2 %pair_side.2 = (bf16[18,256,512]{2,1,0:T(8,128)(2,1)}, bf16[18,256,512]{2,1,0:T(8,128)(2,1)}, bf16[18,384,512]{2,1,0:T(8,128)(2,1)}) custom-call(s32[1]{0:T(128)} %bitcast.refs_0_, bf16[12,128,512]{2,1,0:T(8,128)(2,1)} %collective-permute-done.2.refs_1_.refs_3_.refs_4_, bf16[256,1152]{1,0:T(8,128)(2,1)} %copy.28.refs_1_.refs_2_.refs_4_.refs_7_, ...), custom_call_target="tpu_custom_call" | custom-call | tf_op jit(solution)/shard_map/pair_side/pallas_call | solution.py:228
  78.4 1.0 slice_bitcast_fusion
  79.4 0.1 pad_maximum_fusion.1
  79.5 1.0 copy.27.refs_5_
  80.5 5.3 %key_back.2 = bf16[8,128,512]{2,1,0:T(8,128)(2,1)} custom-call(bf16[18,256,512]{2,1,0:T(8,128)(2,1)} %get-tuple-element.47.refs_12_.grad_ref, bf16[384,768]{1,0:T(8,128)(2,1)} %bitcast.47), custom_call_target="tpu_custom_call" | custom-call | tf_op jit(solution)/shard_map/key_back/pallas_call | solution.py:280
  85.9 8.8 %own_side.3 = (bf16[18,256,512]{2,1,0:T(8,128)(2,1)}, bf16[18,512,256]{2,1,0:T(8,128)(2,1)}, bf16[18,512,256]{2,1,0:T(8,128)(2,1)}, bf16[18,384,512]{2,1,0:T(8,128)(2,1)}) custom-call(bf16[3,128,512]{2,1,0:T(8,128)(2,1)} %collective-permute-done.4.refs_0_, ...), custom_call_target="tpu_custom_call", output_to_operand_aliasing={{0}: (6, {}), {1}: (7, {}), {2}: (8, {}), {3}: (9, {})} | custom-call | tf_op jit(solution)/shard_map/own_side/pallas_call | solution.py:130
  94.7 0.0 collective-permute-done.refs_1_
  94.7 0.0 collective-permute-done.3.refs_6_
  94.7 0.0 copy-start.7
  94.7 0.7 copy-done.7
  95.4 23.5 %pair_side.3 = (bf16[18,256,512]{2,1,0:T(8,128)(2,1)}, bf16[18,256,512]{2,1,0:T(8,128)(2,1)}, bf16[18,384,512]{2,1,0:T(8,128)(2,1)}) custom-call(s32[1]{0:T(128)} %bitcast.refs_0_, bf16[2,128,512]{2,1,0:T(8,128)(2,1)} %collective-permute-done.refs_1_, ...), custom_call_target="tpu_custom_call", output_to_operand_aliasing={{0}: (11, {}), {1}: (12, {}), {2}: (13, {})} | custom-call | tf_op jit(solution)/shard_map/pair_side/pallas_call | solution.py:228
  118.9 5.3 %key_back.3 = bf16[8,128,512]{2,1,0:T(8,128)(2,1)} custom-call(bf16[18,256,512]{2,1,0:T(8,128)(2,1)} %get-tuple-element.51.grad_ref.key_ref, bf16[384,768]{1,0:T(8,128)(2,1)} %bitcast.48), custom_call_target="tpu_custom_call" | custom-call | tf_op jit(solution)/shard_map/key_back/pallas_call | solution.py:280
  124.3 0.0 collective-permute-start.7
  124.3 0.0 copy-start.6
  124.3 16.7 %weight_term.1 = bf16[9,256,128]{2,1,0:T(8,128)(2,1)} custom-call(bf16[18,256,512]{2,1,0:T(8,128)(2,1)} %get-tuple-element.55.query_ref.grad_ref, bf16[18,256,512]{2,1,0:T(8,128)(2,1)} %get-tuple-element.51.grad_ref.key_ref, bf16[18,384,512]{2,1,0:T(8,128)(2,1)} %get-tuple-element.52.own_ref, bf16[18,384,512]{2,1,0:T(8,128)(2,1)} %get-tuple-element.53.partner_ref), custom_call_target="tpu_custom_call" | custom-call | tf_op jit(solution)/shard_map/weight_term/pallas_call | solution.py:355
  141.0 8.2 %collective-permute-done.7.outer_ref = bf16[8,128,512]{2,1,0:T(8,128)(2,1)} collective-permute-done((bf16[8,128,512]{2,1,0:T(8,128)(2,1)}, bf16[8,128,512]{2,1,0:T(8,128)(2,1)}, u32[]{:S(2)}, u32[]{:S(2)}) %collective-permute-start.7) | collective-permute-done | bytes 1048608 | tf_op jit(solution)/shard_map/ppermute | solution.py:369
  149.2 1.2 reshape.30
  150.4 22.9 %all_to_all.10 = bf16[128,18,128]{2,1,0:T(8,128)(2,1)S(1)} all-to-all(bf16[128,18,128]{2,1,0:T(8,128)(2,1)S(1)} %reshape.30), channel_id=1, replica_groups=mesh['cam'=32,'band'=4] {'cam','band'}, dimensions={0} | all-to-all | bytes 1179648 | tf_op jit(solution)/shard_map/all_to_all | solution.py:399
  173.3 0.2 reduce_sum.22
  173.5 0.1 broadcast_in_dim.22
  173.6 20.3 %all_to_all.11 = bf16[128,18,128]{2,1,0:T(8,128)(2,1)S(1)} all-to-all(bf16[128,18,128]{2,1,0:T(8,128)(2,1)S(1)} %broadcast_in_dim.22), channel_id=1, replica_groups=mesh['cam'=32,'band'=4] {'cam','band'}, dimensions={0} | all-to-all | bytes 1179648 | tf_op jit(solution)/shard_map/all_to_all | solution.py:402
  193.9 9.6 %image_back.1 = f32[16,128,512]{2,1,0:T(8,128)} custom-call(bf16[18,256,512]{2,1,0:T(8,128)(2,1)} %get-tuple-element.55.query_ref.grad_ref, bf16[384,768]{1,0:T(8,128)(2,1)} %bitcast.49, bf16[8,128,512]{2,1,0:T(8,128)(2,1)} %copy-done.6, bf16[8,128,512]{2,1,0:T(8,128)(2,1)} %collective-permute-done.7.outer_ref), custom_call_target="tpu_custom_call" | custom-call | tf_op jit(solution)/shard_map/image_back/pallas_call | solution.py:311
  203.5 6.6 %copy.30 = f32[1,128,16,512]{3,2,1,0:T(8,128)} copy(f32[1,128,16,512]{3,1,2,0:T(8,128)} %bitcast.46) | data formatting | bytes 8388608
  210.2 0.1 convert_multiply_fusion
  210.3 1.1 mul.11
  (19 shorter events, 0.0 us)
Async XLA Ops:
  3.4 29.1 %copy-start = (bf16[1,128,16,512]{3,1,2,0:T(8,128)(2,1)}, bf16[1,128,16,512]{3,1,2,0:T(8,128)(2,1)S(1)}, u32[]{:S(2)}) copy-start(bf16[1,128,16,512]{3,1,2,0:T(8,128)(2,1)S(1)} %copy.35) | copy-start | bytes 6291460
  3.4 27.7 %copy-start.1 = (bf16[3,3,256,128]{3,2,1,0:T(8,128)(2,1)S(1)}, bf16[3,3,256,128]{3,2,1,0:T(8,128)(2,1)}, u32[]{:S(2)}) copy-start(bf16[3,3,256,128]{3,2,1,0:T(8,128)(2,1)} %param.5) | copy-start | bytes 1769476
  4.8 45.4 %collective-permute-start.2 = (bf16[12,128,512]{2,1,0:T(8,128)(2,1)}, bf16[12,128,512]{2,1,0:T(8,128)(2,1)}, u32[]{:S(2)}, u32[]{:S(2)}) collective-permute-start(bf16[12,128,512]{2,1,0:T(8,128)(2,1)} %slice.40), channel_id=1, source_target_pairs={{0,124},{4,0},{8,4},{12,8},{16,12},{20,16},{24,20},{28,24},{32,28}... | collective-permute-start | bytes 4718600 | tf_op jit(solution)/shard_map/ppermute | solution.py:369
  13.0 18.1 %copy-start.2 = (bf16[1,1,512,128]{2,3,1,0:T(8,128)(2,1)}, bf16[1,1,512,128]{2,3,1,0:T(8,128)(2,1)S(1)}, u32[]{:S(2)}) copy-start(bf16[1,1,512,128]{2,3,1,0:T(8,128)(2,1)S(1)} %copy.31) | copy-start | bytes 393220
  15.5 62.9 %collective-permute-start.4 = (bf16[3,128,512]{2,1,0:T(8,128)(2,1)}, bf16[3,128,512]{2,1,0:T(8,128)(2,1)}, u32[]{:S(2)}, u32[]{:S(2)}) collective-permute-start(bf16[3,128,512]{2,1,0:T(8,128)(2,1)} %pad_maximum_fusion.2), channel_id=1, source_target_pairs={{0,1},{1,2},{2,3},{4,5},{5,6},{6,7},{8,9},{9,10},{10,11},{12,13},{... | collective-permute-start | bytes 1179656 | tf_op jit(solution)/shard_map/ppermute | solution.py:374
  21.7 9.4 %copy-start.4 = (bf16[1,1,512,128]{2,3,1,0:T(8,128)(2,1)}, bf16[1,1,512,128]{2,3,1,0:T(8,128)(2,1)S(1)}, u32[]{:S(2)}) copy-start(bf16[1,1,512,128]{2,3,1,0:T(8,128)(2,1)S(1)} %copy.32) | copy-start | bytes 393220
  22.5 55.9 %collective-permute-start.5 = (bf16[3,128,512]{2,1,0:T(8,128)(2,1)}, bf16[3,128,512]{2,1,0:T(8,128)(2,1)}, u32[]{:S(2)}, u32[]{:S(2)}) collective-permute-start(bf16[3,128,512]{2,1,0:T(8,128)(2,1)} %pad_maximum_fusion.3), channel_id=1, source_target_pairs={{1,0},{2,1},{3,2},{5,4},{6,5},{7,6},{9,8},{10,9},{11,10},{13,12},{... | collective-permute-start | bytes 1179656 | tf_op jit(solution)/shard_map/ppermute | solution.py:374
  26.2 68.5 %collective-permute-start.1 = (bf16[4,128,512]{2,1,0:T(8,128)(2,1)}, bf16[4,128,512]{2,1,0:T(8,128)(2,1)}, u32[]{:S(2)}, u32[]{:S(2)}) collective-permute-start(bf16[4,128,512]{2,1,0:T(8,128)(2,1)} %pad_maximum_fusion), channel_id=1, source_target_pairs={{0,124},{4,0},{8,4},{12,8},{16,12},{20,16},{24,20},{28,24},{32,28}... | collective-permute-start | bytes 1572872 | tf_op jit(solution)/shard_map/ppermute | solution.py:369
  26.2 68.5 %collective-permute-start = (bf16[2,128,512]{2,1,0:T(8,128)(2,1)}, bf16[2,128,512]{2,1,0:T(8,128)(2,1)}, u32[]{:S(2)}, u32[]{:S(2)}) collective-permute-start(bf16[2,128,512]{2,1,0:T(8,128)(2,1)} %get-tuple-element.65), channel_id=1, source_target_pairs={{4,1},{5,2},{6,3},{8,5},{9,6},{10,7},{12,9},{13,10},{14,11},{16,13... | collective-permute-start | bytes 786440 | tf_op jit(solution)/shard_map/ppermute | solution.py:387
  31.1 18.4 %copy-start.8 = (s32[32]{0:T(128)S(1)}, s32[32]{0:T(128)}, u32[]{:S(2)}) copy-start(s32[32]{0:T(128)} %param.6) | copy-start | bytes 388
  50.2 44.5 %collective-permute-start.3 = (bf16[2,128,512]{2,1,0:T(8,128)(2,1)S(1)}, bf16[2,128,512]{2,1,0:T(8,128)(2,1)S(1)}, u32[]{:S(2)}, u32[]{:S(2)}) collective-permute-start(bf16[2,128,512]{2,1,0:T(8,128)(2,1)S(1)} %get-tuple-element.64), channel_id=1, source_target_pairs={{5,0},{6,1},{7,2},{9,4},{10,5},{11,6},{13,8},{14,9},{15,10},{17,12... | collective-permute-start | bytes 786440 | tf_op jit(solution)/shard_map/ppermute | solution.py:387
  56.2 23.2 %copy-start.3 = (bf16[1,1,512,128]{2,3,1,0:T(8,128)(2,1)S(1)}, bf16[1,1,512,128]{2,3,1,0:T(8,128)(2,1)}, u32[]{:S(2)}) copy-start(bf16[1,1,512,128]{2,3,1,0:T(8,128)(2,1)} %copy-done.2) | copy-start | bytes 393220
  56.2 23.2 %copy-start.5 = (bf16[1,1,512,128]{2,3,1,0:T(8,128)(2,1)S(1)}, bf16[1,1,512,128]{2,3,1,0:T(8,128)(2,1)}, u32[]{:S(2)}) copy-start(bf16[1,1,512,128]{2,3,1,0:T(8,128)(2,1)} %copy-done.4) | copy-start | bytes 393220
  85.9 38.4 %collective-permute-start.6 = (bf16[8,128,512]{2,1,0:T(8,128)(2,1)}, bf16[8,128,512]{2,1,0:T(8,128)(2,1)S(1)}, u32[]{:S(2)}, u32[]{:S(2)}) collective-permute-start(bf16[8,128,512]{2,1,0:T(8,128)(2,1)} %key_back.2), channel_id=1, source_target_pairs={{0,4},{4,8},{8,12},{12,16},{16,20},{20,24},{24,28},{28,32},{32,36}... | collective-permute-start | bytes 3145736 | tf_op jit(solution)/shard_map/ppermute | solution.py:369
  94.7 0.7 copy-start.7
  124.3 24.9 %collective-permute-start.7 = (bf16[8,128,512]{2,1,0:T(8,128)(2,1)}, bf16[8,128,512]{2,1,0:T(8,128)(2,1)}, u32[]{:S(2)}, u32[]{:S(2)}) collective-permute-start(bf16[8,128,512]{2,1,0:T(8,128)(2,1)} %key_back.3), channel_id=1, source_target_pairs={{0,4},{4,8},{8,12},{12,16},{16,20},{20,24},{24,28},{28,32},{32,36}... | collective-permute-start | bytes 3145736 | tf_op jit(solution)/shard_map/ppermute | solution.py:369
  124.3 16.7 %copy-start.6 = (bf16[8,128,512]{2,1,0:T(8,128)(2,1)}, bf16[8,128,512]{2,1,0:T(8,128)(2,1)S(1)}, u32[]{:S(2)}) copy-start(bf16[8,128,512]{2,1,0:T(8,128)(2,1)S(1)} %collective-permute-done.6.inner_ref) | copy-start | bytes 3145732

commit v2 on v1

--- a/solution.py
+++ b/solution.py
@@ -95,21 +95,22 @@
     feat_ref, featt_ref, skew_ref, tap_ref, taps, row = refs[count + 2 + carried :]
     r = pl.program_id(0)
     next_row(pieces, x_refs, taps, row, r)
-    feat = conv_row(weight_ref, taps)
-    feat_ref[0] = feat.astype(BF16)
-    featt_ref[0] = feat.T.astype(BF16)
-    tap_ref[0] = taps[1]
     rows = lax.broadcasted_iota(jnp.int32, (DISP, DISP), 0)
     cols = lax.broadcasted_iota(jnp.int32, (DISP, DISP), 1)
     exchange = jnp.where(rows + cols == DISP - 1, 1.0, 0.0).astype(BF16)
     flipped = jnp.dot(cot_ref[0], exchange, preferred_element_type=F32)
+    feat = conv_row(weight_ref, taps)
     blocks = flipped.shape[0] // DISP
+    skewed = []
     for b in range(blocks):
         part = flipped[b * DISP : (b + 1) * DISP]
         wide = jnp.concatenate([part, jnp.zeros_like(part)], axis=1)
-        skew_ref[0, b * DISP : (b + 1) * DISP] = pltpu.roll(
-            wide, 1, 1, stride=1, stride_axis=0
-        ).astype(BF16)
+        skewed.append(pltpu.roll(wide, 1, 1, stride=1, stride_axis=0).astype(BF16))
+    feat_ref[0] = feat.astype(BF16)
+    featt_ref[0] = feat.T.astype(BF16)
+    for b in range(blocks):
+        skew_ref[0, b * DISP : (b + 1) * DISP] = skewed[b]
+    tap_ref[0] = taps[1]
 
 
 def own_side(pieces, parts, weight_fwd, cot, rows, place, cot_place, carried):
@@ -163,25 +164,36 @@
     columns = blocks * DISP
     offset = off_ref[0]
     scale = 1.0 / math.sqrt(C_OUT)
+    next_row(pieces, x_refs, taps, row, r)
     keyed = keys[...]
-    next_row(pieces, x_refs, taps, row, r)
+    windows = [keyed[:, b * DISP : (b + 2) * DISP] for b in range(blocks)]
+    here = [slice(b * DISP, (b + 1) * DISP) for b in range(blocks)]
+    products = [
+        jnp.dot(featt_ref[0, here[b], :], windows[b], preferred_element_type=F32)
+        for b in range(blocks)
+    ]
     feat = conv_row(weight_ref, taps).astype(BF16).astype(F32)
 
-    heads, tails = [], []
-    for b in range(blocks):
-        here = slice(b * DISP, (b + 1) * DISP)
-        window = keyed[:, b * DISP : (b + 2) * DISP]
-        products = jnp.dot(featt_ref[0, here, :], window, preferred_element_type=F32)
-        squashed = jnp.tanh(products * scale)
-        placed = (
-            skew_ref[0, here, :].astype(F32) * (1.0 - squashed * squashed) * scale
+    placed = []
+    for b in range(blocks):
+        squashed = jnp.tanh(products[b] * scale)
+        placed.append(
+            (skew_ref[0, here[b], :].astype(F32) * (1.0 - squashed * squashed) * scale).astype(
+                BF16
+            )
+        )
+    queries = [
+        lax.dot_general(
+            windows[b], placed[b], (((1,), (1,)), ((), ())), preferred_element_type=F32
         ).astype(BF16)
-        query_ref[0, :, here] = lax.dot_general(
-            window, placed, (((1,), (1,)), ((), ())), preferred_element_type=F32
-        ).astype(BF16)
-        grad = jnp.dot(feat_ref[0, :, here], placed, preferred_element_type=F32)
-        heads.append(grad[:, :DISP])
-        tails.append(grad[:, DISP:])
+        for b in range(blocks)
+    ]
+    grads = [
+        jnp.dot(feat_ref[0, :, here[b]], placed[b], preferred_element_type=F32)
+        for b in range(blocks)
+    ]
+    heads = [grad[:, :DISP] for grad in grads]
+    tails = [grad[:, DISP:] for grad in grads]
     back = jnp.where(offset == 0, 0, DISP - offset)
     lane = lax.broadcasted_iota(jnp.int32, (C_OUT, DISP), 1)
     moved = []
@@ -189,20 +201,19 @@
         tile = tails[b] if b == blocks - 1 else tails[b] + heads[b + 1]
         moved.append(pltpu.roll(tile, back, 1))
     moved.append(jnp.zeros_like(moved[0]))
-    for b in range(blocks):
-        key_ref[0, :, b * DISP : (b + 1) * DISP] = jnp.where(
+    shifted = [jnp.zeros((C_OUT, DISP), F32)]
+    for b in range(blocks):
+        shifted.append(pltpu.roll(feat[:, here[b]], offset, 1))
+    for b in range(blocks):
+        query_ref[0, :, here[b]] = queries[b]
+        key_ref[0, :, here[b]] = jnp.where(
             lane < DISP - offset, moved[b], moved[b + 1]
         ).astype(BF16)
     tap_ref[0] = taps[0]
-
-    empty = jnp.zeros((C_OUT, DISP), F32)
-    moved = [empty]
-    for b in range(blocks):
-        moved.append(pltpu.roll(feat[:, b * DISP : (b + 1) * DISP], offset, 1))
-    keys[:, :DISP] = empty.astype(BF16)
+    keys[:, :DISP] = jnp.zeros((C_OUT, DISP), BF16)
     for b in range(blocks):
         keys[:, (b + 1) * DISP : (b + 2) * DISP] = jnp.where(
-            lane >= offset, moved[b + 1], moved[b]
+            lane >= offset, shifted[b + 1], shifted[b]
         ).astype(BF16)
 
 
@@ -288,41 +299,32 @@
     )(key, weight_bwd)
 
 
-def image_back_kernel(grad_ref, weight_ref, inner_ref, outer_ref, out_ref):
-    s = pl.program_id(0)
-    inside = (s > 0) & (s < pl.num_programs(0) - 1)
+def image_back_kernel(grad_ref, weight_ref, recv_ref, *rest):
+    out_ref = rest[-1]
     for r in range(GROUP):
-        out_ref[r] = back_row(weight_ref, grad_ref, r)
-
-    @pl.when(inside)
-    def _():
-        out_ref[...] += inner_ref[...].astype(F32)
-
-    @pl.when(jnp.logical_not(inside))
-    def _():
-        out_ref[...] += outer_ref[...].astype(F32)
-
-
-def image_back(query, weight_bwd, inner, outer):
+        out_ref[r] = back_row(weight_ref, grad_ref, r) + recv_ref[r].astype(F32)
+
+
+def image_back(query, weight_bwd, received, first, step, carried):
     rows, _, columns = query.shape
-    count = rows - 2
-    groups = count // GROUP
     block = (GROUP, C_IN, columns)
-    out = pl.pallas_call(
+    operands = [query, weight_bwd, received, *carried]
+    in_specs = [
+        window(C_OUT, columns, first, step),
+        whole(weight_bwd),
+        pl.BlockSpec(block, lambda s: (s, 0, 0)),
+    ]
+    in_specs += [pl.BlockSpec(memory_space=pl.ANY) for _ in carried]
+    return pl.pallas_call(
         image_back_kernel,
-        grid=(groups,),
-        in_specs=[
-            window(C_OUT, columns),
-            whole(weight_bwd),
-            pl.BlockSpec(block, lambda s: (jnp.clip(s - 1, 0, groups - 3), 0, 0)),
-            pl.BlockSpec(block, lambda s: (s // (groups - 1), 0, 0)),
-        ],
-        out_specs=pl.BlockSpec(block, lambda s: (s, 0, 0)),
-        out_shape=jax.ShapeDtypeStruct((count, C_IN, columns), F32),
+        grid=(received.shape[0] // GROUP,),
+        in_specs=in_specs,
+        out_specs=pl.BlockSpec(block, lambda s: ((s * step + first) // GROUP, 0, 0)),
+        out_shape=jax.ShapeDtypeStruct((rows - 2, C_IN, columns), F32),
+        input_output_aliases={3: 0} if carried else {},
         compiler_params=params(),
         name="image_back",
-    )(query, weight_bwd, inner, outer)
-    return jnp.transpose(out, (1, 0, 2))
+    )(*operands)
 
 
 def weight_kernel(query_ref, key_ref, own_ref, partner_ref, out_ref, acc):
@@ -455,13 +457,15 @@
     sent_outer = passed_along(outer_back, "cam", 1)
     key, sent_inner, _ = lax.optimization_barrier((key, sent_inner, outer_back))
     term = weight_term(query, key, own_taps, partner_taps)
-    term, sent_outer = lax.optimization_barrier((term, sent_outer))
+    query, _ = lax.optimization_barrier((query, term))
+    image_grad = image_back(query, weight_bwd, sent_inner, GROUP, GROUP, ())
+    term, sent_outer, image_grad = lax.optimization_barrier((term, sent_outer, image_grad))
     total = summed_everywhere(term)
     normalizer = 1.0 / math.sqrt(lax.axis_size("cam") * lax.axis_size("band") * rows * columns)
     weight_grad = total.astype(F32).reshape(weight.shape) * normalizer
     query, total = lax.optimization_barrier((query, total))
-    image_grad = image_back(query, weight_bwd, sent_inner, sent_outer)
-    return (image_grad[None], weight_grad)
+    image_grad = image_back(query, weight_bwd, sent_outer, 0, rows - GROUP, (image_grad,))
+    return (jnp.transpose(image_grad, (1, 0, 2))[None], weight_grad)
 
 
 def solution(mesh):

time: 212 us -> 195 us (0.920)
  Pallas kernels: 107 us -> 95.1 us
  waiting for transfers between devices: 8.21 us -> 1.87 us
    pallas_call x2, Pallas kernels: 45.7 us -> 33 us  [pair_side(): pl.pallas_call(lambda *refs: pair_kernel(pieces, len(carried), *refs), gr...]
    ppermute x4, waiting for transfers between devices: 8.2 us -> 1.86 us  [passed_along(): return lax.ppermute(x, axis, [(i, (i + by) % size) for i in range(size)])]
    pallas_call x1 -> x2, Pallas kernels: 9.63 us -> 11.5 us  [image_back(): pl.pallas_call(image_back_kernel, grid=(received.shape[0] // GROUP,), in_...]
    unnamed x24 -> x28, local copies, waits for them, and re-layouts: 11.5 us -> 11.5 us
where the time goes in v2:
time: 195 us; the launch traced here: 194 us
  Pallas kernels  95.1 us (49%)
  blocking collectives  44.7 us (23%)
  starting transfers between devices  26.5 us (14%)
  local copies, waits for them, and re-layouts  19.7 us (10%)
  other arithmetic  5.34 us (3%)
    pallas_call x2, Pallas kernels, pair_side(): pl.pallas_call(lambda *refs: pair_kernel(pieces, len(carried), *refs), gr...  33 us
    all_to_all x1, blocking collectives, summed_everywhere(): mine = lax.all_to_all(pieces, axes, split_axis=0, concat_axis=0, tiled=True)  24.4 us
    pallas_call x2, Pallas kernels, own_side(): pl.pallas_call(lambda *refs: own_kernel(pieces, len(carried), *refs), gri...  23.2 us
    all_to_all x1, blocking collectives, summed_everywhere(): return lax.all_to_all(spread, axes, split_axis=0, concat_axis=0, tiled=True)  20.3 us
    pallas_call x1, Pallas kernels, weight_term(): pl.pallas_call(weight_kernel, grid=((rows - 2) // GROUP,), in_specs=[grad...  16.7 us
    unnamed x28, local copies, waits for them, and re-layouts  11.5 us
    pallas_call x2, Pallas kernels, image_back(): pl.pallas_call(image_back_kernel, grid=(received.shape[0] // GROUP,), in_...  11.5 us
    ppermute x2, starting transfers between devices, diagonal(): return lax.ppermute(x, ('cam', 'band'), pairs)  11.4 us
  transfers between devices with their start and end apart: 8, of which 1 were waited for; matrix products, arithmetic and copies ran while one was open for 6% of the time, Pallas kernels for 46%

profile of v2, /device:TPU:1, one launch (start us, length us, event | category | flops | bytes accessed | tf_op | source)
XLA Modules:
  0.0 194.1 jit_solution(6216763705386323028)
XLA Ops:
  0.6 2.8 %copy.36 = bf16[1,128,16,512]{3,1,2,0:T(8,128)(2,1)S(1)} copy(bf16[1,128,16,512]{3,2,1,0:T(8,128)(2,1)} %param.4) | data formatting | bytes 4194304 | tf_op args[0]
  3.4 0.0 copy-start
  3.4 0.0 copy-start.2
  3.4 1.4 slice.40
  4.8 7.1 %collective-permute-start.2 = (bf16[12,128,512]{2,1,0:T(8,128)(2,1)}, bf16[12,128,512]{2,1,0:T(8,128)(2,1)}, u32[]{:S(2)}, u32[]{:S(2)}) collective-permute-start(bf16[12,128,512]{2,1,0:T(8,128)(2,1)} %slice.40), channel_id=1, source_target_pairs={{0,124},{4,0},{8,4},{12,8},{16,12},{20,16},{24,20},{28,24},{32,28}... | collective-permute-start | bytes 4718600 | tf_op jit(solution)/shard_map/ppermute | solution.py:371
  11.9 1.0 fusion.1
  12.9 0.1 copy.32
  13.0 0.8 fusion.2
  13.8 1.8 pad_maximum_fusion.2
  15.5 6.0 %collective-permute-start.4 = (bf16[3,128,512]{2,1,0:T(8,128)(2,1)}, bf16[3,128,512]{2,1,0:T(8,128)(2,1)}, u32[]{:S(2)}, u32[]{:S(2)}) collective-permute-start(bf16[3,128,512]{2,1,0:T(8,128)(2,1)} %pad_maximum_fusion.2), channel_id=1, source_target_pairs={{0,1},{1,2},{2,3},{4,5},{5,6},{6,7},{8,9},{9,10},{10,11},{12,13},{... | collective-permute-start | bytes 1179656 | tf_op jit(solution)/shard_map/ppermute | solution.py:376
  21.6 0.1 copy.33
  21.7 0.8 pad_maximum_fusion.3
  22.5 1.9 collective-permute-start.5
  24.4 1.8 pad_maximum_fusion
  26.2 4.9 %collective-permute-start = (bf16[2,128,512]{2,1,0:T(8,128)(2,1)}, bf16[2,128,512]{2,1,0:T(8,128)(2,1)}, u32[]{:S(2)}, u32[]{:S(2)}) collective-permute-start(bf16[2,128,512]{2,1,0:T(8,128)(2,1)} %get-tuple-element.69), channel_id=1, source_target_pairs={{4,1},{5,2},{6,3},{8,5},{9,6},{10,7},{12,9},{13,10},{14,11},{16,13... | collective-permute-start | bytes 786440 | tf_op jit(solution)/shard_map/ppermute | solution.py:389
  31.1 0.2 copy.22
  31.4 0.0 copy-start.10
  31.4 1.1 copy.29.refs_1_.refs_2_.refs_4_.refs_7_
  32.5 0.7 copy.30
  33.1 0.9 copy.34
  34.0 14.9 %own_side.2 = (bf16[18,256,512]{2,1,0:T(8,128)(2,1)}, bf16[18,512,256]{2,1,0:T(8,128)(2,1)}, bf16[18,512,256]{2,1,0:T(8,128)(2,1)}, bf16[18,384,512]{2,1,0:T(8,128)(2,1)}) custom-call(bf16[16,128,512]{2,1,0:T(8,128)(2,1)} %bitcast.43, bf16[256,1152]{1,0:T(8,128)(2,1)} %copy.29.refs_1_.refs_2_.refs_4_.refs_7_, bf16[16,512,128]{2,1,0:T(8,128)(2,1)} %bitcast.52), custom_call_target="tpu_custom_call" | custom-call | tf_op jit(solution)/shard_map/own_side/pallas_call | solution.py:131
  49.0 0.6 fusion
  49.6 0.0 collective-permute-done.2.refs_1_.refs_3_.refs_4_
  49.6 6.6 %collective-permute-start.3 = (bf16[2,128,512]{2,1,0:T(8,128)(2,1)S(1)}, bf16[2,128,512]{2,1,0:T(8,128)(2,1)S(1)}, u32[]{:S(2)}, u32[]{:S(2)}) collective-permute-start(bf16[2,128,512]{2,1,0:T(8,128)(2,1)S(1)} %get-tuple-element.68), channel_id=1, source_target_pairs={{5,0},{6,1},{7,2},{9,4},{10,5},{11,6},{13,8},{14,9},{15,10},{17,12... | collective-permute-start | bytes 786440 | tf_op jit(solution)/shard_map/ppermute | solution.py:389
  56.3 16.2 %pair_side.2 = (bf16[18,256,512]{2,1,0:T(8,128)(2,1)}, bf16[18,256,512]{2,1,0:T(8,128)(2,1)}, bf16[18,384,512]{2,1,0:T(8,128)(2,1)}) custom-call(s32[1]{0:T(128)} %bitcast.refs_0_, bf16[12,128,512]{2,1,0:T(8,128)(2,1)} %collective-permute-done.2.refs_1_.refs_3_.refs_4_, bf16[256,1152]{1,0:T(8,128)(2,1)} %copy.29.refs_1_.refs_2_.refs_4_.refs_7_, ...), custom_call_target="tpu_custom_call" | custom-call | tf_op jit(solution)/shard_map/pair_side/pallas_call | solution.py:239
  72.5 1.0 slice_bitcast_fusion
  73.5 0.1 pad_maximum_fusion.1
  73.6 1.0 copy.28.refs_5_
  74.6 5.4 %key_back.2 = bf16[8,128,512]{2,1,0:T(8,128)(2,1)} custom-call(bf16[18,256,512]{2,1,0:T(8,128)(2,1)} %get-tuple-element.49.refs_12_.grad_ref, bf16[384,768]{1,0:T(8,128)(2,1)} %bitcast.47), custom_call_target="tpu_custom_call" | custom-call | tf_op jit(solution)/shard_map/key_back/pallas_call | solution.py:291
  79.9 8.3 %own_side.3 = (bf16[18,256,512]{2,1,0:T(8,128)(2,1)}, bf16[18,512,256]{2,1,0:T(8,128)(2,1)}, bf16[18,512,256]{2,1,0:T(8,128)(2,1)}, bf16[18,384,512]{2,1,0:T(8,128)(2,1)}) custom-call(bf16[3,128,512]{2,1,0:T(8,128)(2,1)} %collective-permute-done.4.refs_0_, ...), custom_call_target="tpu_custom_call", output_to_operand_aliasing={{0}: (6, {}), {1}: (7, {}), {2}: (8, {}), {3}: (9, {})} | custom-call | tf_op jit(solution)/shard_map/own_side/pallas_call | solution.py:131
  88.2 0.0 copy-start.9
  88.3 0.7 copy-done.9
  89.0 16.8 %pair_side.3 = (bf16[18,256,512]{2,1,0:T(8,128)(2,1)}, bf16[18,256,512]{2,1,0:T(8,128)(2,1)}, bf16[18,384,512]{2,1,0:T(8,128)(2,1)}) custom-call(s32[1]{0:T(128)} %bitcast.refs_0_, bf16[2,128,512]{2,1,0:T(8,128)(2,1)} %collective-permute-done.refs_1_, ...), custom_call_target="tpu_custom_call", output_to_operand_aliasing={{0}: (11, {}), {1}: (12, {}), {2}: (13, {})} | custom-call | tf_op jit(solution)/shard_map/pair_side/pallas_call | solution.py:239
  105.7 5.3 %key_back.3 = bf16[8,128,512]{2,1,0:T(8,128)(2,1)} custom-call(bf16[18,256,512]{2,1,0:T(8,128)(2,1)} %get-tuple-element.53.grad_ref.key_ref, bf16[384,768]{1,0:T(8,128)(2,1)} %bitcast.48), custom_call_target="tpu_custom_call" | custom-call | tf_op jit(solution)/shard_map/key_back/pallas_call | solution.py:291
  111.1 0.0 collective-permute-start.7
  111.1 0.0 copy-start.8
  111.1 16.7 %weight_term.1 = bf16[9,256,128]{2,1,0:T(8,128)(2,1)} custom-call(bf16[18,256,512]{2,1,0:T(8,128)(2,1)} %get-tuple-element.59.query_ref.grad_ref, bf16[18,256,512]{2,1,0:T(8,128)(2,1)} %get-tuple-element.53.grad_ref.key_ref, bf16[18,384,512]{2,1,0:T(8,128)(2,1)} %get-tuple-element.54.own_ref, bf16[18,384,512]{2,1,0:T(8,128)(2,1)} %get-tuple-element.55.partner_ref), custom_call_target="tpu_custom_call" | custom-call | tf_op jit(solution)/shard_map/weight_term/pallas_call | solution.py:357
  127.8 5.8 %image_back.2.rest_0_ = f32[16,128,512]{2,1,0:T(8,128)} custom-call(bf16[18,256,512]{2,1,0:T(8,128)(2,1)} %get-tuple-element.59.query_ref.grad_ref, bf16[384,768]{1,0:T(8,128)(2,1)} %bitcast.49, bf16[8,128,512]{2,1,0:T(8,128)(2,1)} %copy-done.8), custom_call_target="tpu_custom_call" | custom-call | tf_op jit(solution)/shard_map/image_back/pallas_call | solution.py:318
  133.5 1.9 collective-permute-done.7.recv_ref
  135.4 0.2 reshape.30
  135.6 24.4 %all_to_all.10 = bf16[128,18,128]{2,1,0:T(8,128)(2,1)S(1)} all-to-all(bf16[128,18,128]{2,1,0:T(8,128)(2,1)S(1)} %reshape.30), channel_id=1, replica_groups=mesh['cam'=32,'band'=4] {'cam','band'}, dimensions={0} | all-to-all | bytes 1179648 | tf_op jit(solution)/shard_map/all_to_all | solution.py:401
  160.0 0.2 reduce_sum.22
  160.2 0.1 broadcast_in_dim.22
  160.3 20.3 %all_to_all.11 = bf16[128,18,128]{2,1,0:T(8,128)(2,1)S(1)} all-to-all(bf16[128,18,128]{2,1,0:T(8,128)(2,1)S(1)} %broadcast_in_dim.22), channel_id=1, replica_groups=mesh['cam'=32,'band'=4] {'cam','band'}, dimensions={0} | all-to-all | bytes 1179648 | tf_op jit(solution)/shard_map/all_to_all | solution.py:404
  180.6 5.7 %image_back.3 = f32[16,128,512]{2,1,0:T(8,128)} custom-call(bf16[18,256,512]{2,1,0:T(8,128)(2,1)} %get-tuple-element.59.query_ref.grad_ref, bf16[384,768]{1,0:T(8,128)(2,1)} %bitcast.50, bf16[8,128,512]{2,1,0:T(8,128)(2,1)} %copy-done.7, f32[16,128,512]{2,1,0:T(8,128)} %image_back.2.rest_0_), custom_call_target="tpu_custom_call", output_to_operand_aliasing={{}: (3, {})} | custom-call | tf_op jit(solution)/shard_map/image_back/pallas_call | solution.py:318
  186.3 6.6 %copy.31 = f32[1,128,16,512]{3,2,1,0:T(8,128)} copy(f32[1,128,16,512]{3,1,2,0:T(8,128)} %bitcast.46) | data formatting | bytes 8388608
  192.9 0.1 convert_multiply_fusion
  193.0 1.1 mul.11
  (24 shorter events, 0.1 us)
Async XLA Ops:
  3.4 28.0 %copy-start = (bf16[1,128,16,512]{3,1,2,0:T(8,128)(2,1)}, bf16[1,128,16,512]{3,1,2,0:T(8,128)(2,1)S(1)}, u32[]{:S(2)}) copy-start(bf16[1,128,16,512]{3,1,2,0:T(8,128)(2,1)S(1)} %copy.36) | copy-start | bytes 6291460
  3.4 27.7 %copy-start.2 = (bf16[3,3,256,128]{3,2,1,0:T(8,128)(2,1)S(1)}, bf16[3,3,256,128]{3,2,1,0:T(8,128)(2,1)}, u32[]{:S(2)}) copy-start(bf16[3,3,256,128]{3,2,1,0:T(8,128)(2,1)} %param.5) | copy-start | bytes 1769476
  4.8 44.9 %collective-permute-start.2 = (bf16[12,128,512]{2,1,0:T(8,128)(2,1)}, bf16[12,128,512]{2,1,0:T(8,128)(2,1)}, u32[]{:S(2)}, u32[]{:S(2)}) collective-permute-start(bf16[12,128,512]{2,1,0:T(8,128)(2,1)} %slice.40), channel_id=1, source_target_pairs={{0,124},{4,0},{8,4},{12,8},{16,12},{20,16},{24,20},{28,24},{32,28}... | collective-permute-start | bytes 4718600 | tf_op jit(solution)/shard_map/ppermute | solution.py:371
  13.0 18.1 %copy-start.3 = (bf16[1,1,512,128]{2,3,1,0:T(8,128)(2,1)}, bf16[1,1,512,128]{2,3,1,0:T(8,128)(2,1)S(1)}, u32[]{:S(2)}) copy-start(bf16[1,1,512,128]{2,3,1,0:T(8,128)(2,1)S(1)} %copy.32) | copy-start | bytes 393220
  15.5 56.9 %collective-permute-start.4 = (bf16[3,128,512]{2,1,0:T(8,128)(2,1)}, bf16[3,128,512]{2,1,0:T(8,128)(2,1)}, u32[]{:S(2)}, u32[]{:S(2)}) collective-permute-start(bf16[3,128,512]{2,1,0:T(8,128)(2,1)} %pad_maximum_fusion.2), channel_id=1, source_target_pairs={{0,1},{1,2},{2,3},{4,5},{5,6},{6,7},{8,9},{9,10},{10,11},{12,13},{... | collective-permute-start | bytes 1179656 | tf_op jit(solution)/shard_map/ppermute | solution.py:376
  21.7 9.4 %copy-start.5 = (bf16[1,1,512,128]{2,3,1,0:T(8,128)(2,1)}, bf16[1,1,512,128]{2,3,1,0:T(8,128)(2,1)S(1)}, u32[]{:S(2)}) copy-start(bf16[1,1,512,128]{2,3,1,0:T(8,128)(2,1)S(1)} %copy.33) | copy-start | bytes 393220
  22.5 50.0 %collective-permute-start.5 = (bf16[3,128,512]{2,1,0:T(8,128)(2,1)}, bf16[3,128,512]{2,1,0:T(8,128)(2,1)}, u32[]{:S(2)}, u32[]{:S(2)}) collective-permute-start(bf16[3,128,512]{2,1,0:T(8,128)(2,1)} %pad_maximum_fusion.3), channel_id=1, source_target_pairs={{1,0},{2,1},{3,2},{5,4},{6,5},{7,6},{9,8},{10,9},{11,10},{13,12},{... | collective-permute-start | bytes 1179656 | tf_op jit(solution)/shard_map/ppermute | solution.py:376
  26.2 62.0 %collective-permute-start.1 = (bf16[4,128,512]{2,1,0:T(8,128)(2,1)}, bf16[4,128,512]{2,1,0:T(8,128)(2,1)}, u32[]{:S(2)}, u32[]{:S(2)}) collective-permute-start(bf16[4,128,512]{2,1,0:T(8,128)(2,1)} %pad_maximum_fusion), channel_id=1, source_target_pairs={{0,124},{4,0},{8,4},{12,8},{16,12},{20,16},{24,20},{28,24},{32,28}... | collective-permute-start | bytes 1572872 | tf_op jit(solution)/shard_map/ppermute | solution.py:371
  26.2 62.0 %collective-permute-start = (bf16[2,128,512]{2,1,0:T(8,128)(2,1)}, bf16[2,128,512]{2,1,0:T(8,128)(2,1)}, u32[]{:S(2)}, u32[]{:S(2)}) collective-permute-start(bf16[2,128,512]{2,1,0:T(8,128)(2,1)} %get-tuple-element.69), channel_id=1, source_target_pairs={{4,1},{5,2},{6,3},{8,5},{9,6},{10,7},{12,9},{13,10},{14,11},{16,13... | collective-permute-start | bytes 786440 | tf_op jit(solution)/shard_map/ppermute | solution.py:389
  31.4 17.6 %copy-start.10 = (s32[32]{0:T(128)S(1)}, s32[32]{0:T(128)}, u32[]{:S(2)}) copy-start(s32[32]{0:T(128)} %param.6) | copy-start | bytes 388
  49.6 38.6 %collective-permute-start.3 = (bf16[2,128,512]{2,1,0:T(8,128)(2,1)S(1)}, bf16[2,128,512]{2,1,0:T(8,128)(2,1)S(1)}, u32[]{:S(2)}, u32[]{:S(2)}) collective-permute-start(bf16[2,128,512]{2,1,0:T(8,128)(2,1)S(1)} %get-tuple-element.68), channel_id=1, source_target_pairs={{5,0},{6,1},{7,2},{9,4},{10,5},{11,6},{13,8},{14,9},{15,10},{17,12... | collective-permute-start | bytes 786440 | tf_op jit(solution)/shard_map/ppermute | solution.py:389
  56.2 17.2 %copy-start.4 = (bf16[1,1,512,128]{2,3,1,0:T(8,128)(2,1)S(1)}, bf16[1,1,512,128]{2,3,1,0:T(8,128)(2,1)}, u32[]{:S(2)}) copy-start(bf16[1,1,512,128]{2,3,1,0:T(8,128)(2,1)} %copy-done.3) | copy-start | bytes 393220
  56.2 17.2 %copy-start.6 = (bf16[1,1,512,128]{2,3,1,0:T(8,128)(2,1)S(1)}, bf16[1,1,512,128]{2,3,1,0:T(8,128)(2,1)}, u32[]{:S(2)}) copy-start(bf16[1,1,512,128]{2,3,1,0:T(8,128)(2,1)} %copy-done.5) | copy-start | bytes 393220
  79.9 31.1 %collective-permute-start.6 = (bf16[8,128,512]{2,1,0:T(8,128)(2,1)}, bf16[8,128,512]{2,1,0:T(8,128)(2,1)S(1)}, u32[]{:S(2)}, u32[]{:S(2)}) collective-permute-start(bf16[8,128,512]{2,1,0:T(8,128)(2,1)} %key_back.2), channel_id=1, source_target_pairs={{0,4},{4,8},{8,12},{12,16},{16,20},{20,24},{24,28},{28,32},{32,36}... | collective-permute-start | bytes 3145736 | tf_op jit(solution)/shard_map/ppermute | solution.py:371
  88.2 0.7 copy-start.9
  111.1 24.3 %collective-permute-start.7 = (bf16[8,128,512]{2,1,0:T(8,128)(2,1)}, bf16[8,128,512]{2,1,0:T(8,128)(2,1)S(1)}, u32[]{:S(2)}, u32[]{:S(2)}) collective-permute-start(bf16[8,128,512]{2,1,0:T(8,128)(2,1)} %key_back.3), channel_id=1, source_target_pairs={{0,4},{4,8},{8,12},{12,16},{16,20},{20,24},{24,28},{28,32},{32,36}... | collective-permute-start | bytes 3145736 | tf_op jit(solution)/shard_map/ppermute | solution.py:371
  111.1 16.7 %copy-start.8 = (bf16[8,128,512]{2,1,0:T(8,128)(2,1)}, bf16[8,128,512]{2,1,0:T(8,128)(2,1)S(1)}, u32[]{:S(2)}) copy-start(bf16[8,128,512]{2,1,0:T(8,128)(2,1)S(1)} %collective-permute-done.6.recv_ref) | copy-start | bytes 3145732
  127.8 7.6 %copy-start.1 = (bf16[9,256,128]{2,1,0:T(8,128)(2,1)S(1)}, bf16[9,256,128]{2,1,0:T(8,128)(2,1)}, u32[]{:S(2)}) copy-start(bf16[9,256,128]{2,1,0:T(8,128)(2,1)} %weight_term.1) | copy-start | bytes 1769476
  135.4 45.2 %copy-start.7 = (bf16[8,128,512]{2,1,0:T(8,128)(2,1)}, bf16[8,128,512]{2,1,0:T(8,128)(2,1)S(1)}, u32[]{:S(2)}) copy-start(bf16[8,128,512]{2,1,0:T(8,128)(2,1)S(1)} %collective-permute-done.7.recv_ref) | copy-start | bytes 3145732
